TPU v7x, 256 devices: a whole 4x4x8 slice. The times are simulated.
256 devices in a mesh: member: 64 (over z_lo, x, y, core), shard: 4 (over z_hi).
Axes of the slice: x: 4, y: 4, z: 8 (z_hi: 4, z_lo: 2; z = z_hi * 2 + z_lo), core: 2. Of those that a mesh axis runs over, the one named last changes fastest.
Arguments:
- processor_latent: bfloat16 [64, 128, 1024], P('member', 'shard'), may hold values from -240 to 240
- stencil_index: int32 [4, 3, 768], P('shard'), may hold values from 0 to 127
- interp_weight: float32 [4, 3, 768], P('shard'), may hold values from 0.1 to 1
- prev_state: float32 [4, 112, 768], P('shard'), may hold values from -6 to 6
- observed: float32 [4, 112, 768], P('shard', None, 'member'), may hold values from -6 to 6
- cell_area: float32 [4, 768], P('shard', 'member'), may hold values from 0.5 to 2
- var_weight: float32 [112], replicated, may hold values from 1 to 16
- hidden_weight: bfloat16 [1024, 1024], replicated, may hold values from -0.1875 to 0.1875
- hidden_bias: float32 [1024], replicated, may hold values from -3 to 3
- output_weight: bfloat16 [1024, 112], replicated, may hold values from -0.1875 to 0.1875
- output_bias: float32 [112], replicated, may hold values from -3 to 3
Outputs:
- mesh_grad: float32 [64, 128, 1024], P('member', 'shard')
Inputs may be any that keep to these rules, and one draw needn't show every extreme that they name: `stencil_index`: rows of the same member's mesh.
All inputs are finite; a program needn't handle non-finite values.
Results may differ from a plain program's by a relative error of at most 0.019.
Values may be sent and summed in bfloat16 or wider, within the bound.
A program may use at most 64 MiB of HBM per device.

v0:
```python
import jax
import jax.numpy as jnp
from jax import lax
from jax.sharding import PartitionSpec as P

smoothing = 0.05
fairness = 0.95
epsilon = 1e-05


def softened_slope(differ):
    return differ / jnp.sqrt(differ * differ + smoothing * smoothing)


def normalize(latent):
    average = jnp.mean(latent, axis=1, keepdims=True)
    centred = latent - average
    inverse = lax.rsqrt(jnp.mean(centred * centred, axis=1, keepdims=True) + epsilon)
    return (centred * inverse, inverse)


def stencil_matrix(stencil, weights, row_count):
    row_ids = lax.iota(jnp.int32, row_count)
    hits = stencil[:, :, None] == row_ids[None, None, :]
    return jnp.sum(jnp.where(hits, weights[:, :, None], 0.0), axis=0)


def decode_members(normed, hidden_weight, hidden_bias, output_weight, output_bias, previous):
    pre_act = jnp.dot(normed, hidden_weight, preferred_element_type=jnp.float32) + hidden_bias
    hidden = jax.nn.silu(pre_act).astype(jnp.bfloat16)
    update = lax.dot_general(
        output_weight, hidden, (((0,), (1,)), ((), ())), preferred_element_type=jnp.float32
    )
    return (previous + (update + output_bias[:, None]), pre_act)


def local(
    processor_latent,
    stencil_index,
    interp_weight,
    prev_state,
    observed,
    cell_area,
    var_weight,
    hidden_weight,
    hidden_bias,
    output_weight,
    output_bias,
):
    mesh_local = processor_latent[0]
    stencil = stencil_index[0]
    weights = interp_weight[0]
    previous = prev_state[0]
    cell_count = stencil.shape[1]
    features = mesh_local.shape[1]
    variables = previous.shape[0]
    members = lax.axis_size("member")
    block_cells = cell_count // members
    shard_rows = lax.all_gather(mesh_local, "shard", axis=0, tiled=True)
    matrix = stencil_matrix(stencil, weights, shard_rows.shape[0])
    latent = jnp.dot(
        matrix,
        shard_rows.astype(jnp.float32),
        precision=lax.Precision.HIGHEST,
        preferred_element_type=jnp.float32,
    )
    normal_form, inverse = normalize(latent)
    normed = normal_form.astype(jnp.bfloat16)
    fairness_factor = (1.0 - fairness) / members
    bounds = (0, block_cells)
    arranged = normed.reshape(members, block_cells, features)
    earlier = previous.reshape(variables, members, block_cells)
    first_cell, stop_cell = bounds
    width_part = stop_cell - first_cell
    piece_rows = arranged.reshape(-1, features)
    prior_piece = earlier.reshape(variables, -1)
    prediction_piece, preactivation_piece = decode_members(
        piece_rows, hidden_weight, hidden_bias, output_weight, output_bias, prior_piece
    )
    received = lax.all_to_all(
        prediction_piece[None], "member", split_axis=2, concat_axis=0, tiled=True
    )
    stored = preactivation_piece.reshape(members, width_part, -1)
    pre_act = stored.reshape(cell_count, -1)
    flattened = received.reshape(members, -1)
    groups = flattened.reshape(members // 8, 8, -1)

    def group_pairs(chosen):
        return jnp.sum(softened_slope(chosen[:, None] - flattened[None]), axis=1)

    pairwise_sums = lax.map(group_pairs, groups).reshape(received.shape)
    loss_weighting = cell_area[0][None, None, :] * var_weight[None, :, None]
    slopes = (
        loss_weighting
        * (
            softened_slope(received - observed[0][None])
            - (1.0 - fairness_factor) / (members - 1) * pairwise_sums
        )
    ).astype(jnp.bfloat16)
    upstream_gradient = lax.all_to_all(slopes, "member", split_axis=0, concat_axis=2, tiled=True)[0]
    grad_hidden = lax.dot_general(
        upstream_gradient,
        output_weight,
        (((0,), (1,)), ((), ())),
        preferred_element_type=jnp.float32,
    )
    logistic = jax.nn.sigmoid(pre_act)
    grad_pre = (grad_hidden * (logistic * (1.0 + pre_act * (1.0 - logistic)))).astype(jnp.bfloat16)
    grad_normed = lax.dot_general(
        grad_pre, hidden_weight, (((1,), (1,)), ((), ())), preferred_element_type=jnp.float32
    )
    grad_cell = inverse * (
        grad_normed
        - jnp.mean(grad_normed, axis=1, keepdims=True)
        - normal_form * jnp.mean(grad_normed * normal_form, axis=1, keepdims=True)
    )
    matrix = stencil_matrix(stencil, weights, lax.axis_size("shard") * mesh_local.shape[0])
    mesh_grad = lax.psum_scatter(
        lax.dot_general(
            matrix,
            grad_cell,
            (((0,), (0,)), ((), ())),
            precision=lax.Precision.HIGHEST,
            preferred_element_type=jnp.float32,
        ).astype(jnp.bfloat16),
        "shard",
        scatter_dimension=0,
        tiled=True,
    ).astype(jnp.float32)
    return mesh_grad[None]


def solution(mesh):
    in_specs = (
        P("member", "shard", None),
        P("shard", None, None),
        P("shard", None, None),
        P("shard", None, None),
        P("shard", None, "member"),
        P("shard", "member"),
        P(),
        P(),
        P(),
        P(),
        P(),
    )
    out_specs = P("member", "shard", None)
    return jax.shard_map(local, mesh=mesh, in_specs=in_specs, out_specs=out_specs, check_vma=False)
```

profile of v0, /device:TPU:2, one launch (start us, length us, event | category | flops | bytes accessed | tf_op | source)
XLA Modules:
  0.0 147.1 jit_solution(18232021255405809372)
XLA Ops:
  6.5 0.9 copy.50
  7.4 0.7 copy.51
  8.1 18.1 %all-gather = bf16[1,128,1024]{2,1,0:T(8,128)(2,1)S(1)} all-gather(bf16[1,32,1024]{2,1,0:T(8,128)(2,1)} %param.13), channel_id=2, replica_groups=mesh['member'=64,'shard'=4] {'shard'}, dimensions={1}, use_global_device_ids=true | all-gather | bytes 327680 | tf_op jit(solution)/shard_map/all_gather | solution.py:59
  26.2 0.8 select_reduce_fusion
  27.0 0.7 copy-done.2
  27.7 1.5 %fusion.31 = (f32[768]{0:T(1024)S(1)}, f32[768,1024]{1,0:T(8,128)S(1)}) fusion(f32[768,128]{1,0:T(8,128)S(1)} %select_reduce_fusion, bf16[1,128,1024]{2,1,0:T(8,128)(2,1)S(1)} %all-gather), kind=kOutput, calls=%fused_computation.52 | convolution fusion | flops 1208745216 | bytes 3804160 | tf_op jit(solution)/shard_map/dot_general | solution.py:61
  29.2 0.4 multiply_reduce_fusion.1
  29.8 1.9 %fusion.9 = f32[768,1024]{1,0:T(8,128)S(1)} fusion(bf16[1024,1024]{1,0:T(8,128)(2,1)S(1)} %copy-done, f32[768,1024]{1,0:T(8,128)S(1)} %get-tuple-element.55, f32[768]{0:T(1024)S(1)} %add_rsqrt_fusion, f32[768]{0:T(1024)S(1)} %broadcast_multiply_fusion.4), kind=kOutput, calls=%fused_computation.19 | convolution fusion | flops 1612972032 | bytes 8394752 | tf_op jit(solution)/shard_map/dot_general | solution.py:29
  31.7 1.7 %copy-done.14 = f32[768,1024]{1,0:T(8,128)} copy-done((f32[768,1024]{1,0:T(8,128)}, f32[768,1024]{1,0:T(8,128)S(1)}, u32[]{:S(2)}) %copy-start.14) | copy-done | bytes 3145752
  33.4 1.1 fusion.25
  34.5 1.0 copy.34
  35.5 8.5 %all-to-all-start = ((f32[1,112,768]{1,0,2:T(1,128)}), f32[1,112,768]{1,0,2:T(1,128)S(1)}, u32[]{:S(2)}, u32[]{:S(2)}) async-start(f32[1,112,768]{1,0,2:T(1,128)} %copy.34), calls=%async_computation | async-start | bytes 786432 | tf_op jit(solution)/shard_map/all_to_all | solution.py:80
  44.0 0.0 reduce-scatter.2.cloned.1.call-start
  44.1 0.7 broadcast_multiply_fusion.1
  44.8 8.8 %all-to-all-done = f32[1,112,768]{1,0,2:T(1,128)S(1)} async-done(((f32[1,112,768]{1,0,2:T(1,128)}), f32[1,112,768]{1,0,2:T(1,128)S(1)}, u32[]{:S(2)}, u32[]{:S(2)}) %all-to-all-start) | async-done | bytes 344096 | tf_op jit(solution)/shard_map/all_to_all | solution.py:80
  53.6 3.3 %copy.36 = f32[64,1,112,12]{3,2,0,1:T(8,128)} copy(f32[64,1,112,12]{2,1,3,0:T(1,128)S(1)} %bitcast.64) | data formatting | bytes 688128 | tf_op jit(solution)/shard_map/all_to_all | solution.py:80
  56.9 1.3 copy.40
  58.2 3.8 %reshape_reshape.3 = f32[8,8,1344]{2,1,0:T(8,128)} reshape(f32[64,1,112,12]{3,2,0,1:T(8,128)} %copy.36) | data formatting | bytes 688128 | tf_op jit(solution)/shard_map/reshape;reshape | solution.py:86
  62.0 1.2 sub.126
  63.2 18.5 %while.11 = (s32[]{:T(128)}, f32[8,8,1344]{2,1,0:T(8,128)}, f32[8,8,1344]{2,1,0:T(8,128)}, f32[64,112,12]{0,2,1:T(8,128)}, f32[64,1344]{0,1:T(8,128)S(1)}, /*index=5*/s32[]{:T(128)}) while((s32[]{:T(128)}, f32[8,8,1344]{2,1,0:T(8,128)}, f32[8,8,1344]{2,1,0:T(8,128)}, f32[64,112,12]{0,2,1:T(8,128)}, f32[64,1344]{0,1:T(8,128)S(1)}, ...), condition=%wide.wide.region_5.6_spmd, body=%wide.wide.region_3.5_spmd.sunk | while | flops 3429890 | bytes 1292373 | solution.py:91
  63.3 0.2 copy.55
  63.5 0.8 dynamic-slice_bitcast_fusion.3
  64.3 0.6 fusion.41
  64.9 0.6 bitcast_dynamic-update-slice_fusion.3
  65.6 0.2 copy.55
  65.8 0.8 dynamic-slice_bitcast_fusion.3
  66.6 0.6 fusion.41
  67.3 0.6 bitcast_dynamic-update-slice_fusion.3
  67.9 0.2 copy.55
  68.1 0.8 dynamic-slice_bitcast_fusion.3
  68.9 0.6 fusion.41
  69.6 0.6 bitcast_dynamic-update-slice_fusion.3
  70.2 0.2 copy.55
  70.4 0.8 dynamic-slice_bitcast_fusion.3
  71.2 0.6 fusion.41
  71.9 0.6 bitcast_dynamic-update-slice_fusion.3
  72.5 0.2 copy.55
  72.7 0.8 dynamic-slice_bitcast_fusion.3
  73.5 0.6 fusion.41
  74.2 0.6 bitcast_dynamic-update-slice_fusion.3
  74.8 0.2 copy.55
  75.0 0.8 dynamic-slice_bitcast_fusion.3
  75.8 0.6 fusion.41
  76.5 0.6 bitcast_dynamic-update-slice_fusion.3
  77.1 0.2 copy.55
  77.4 0.8 dynamic-slice_bitcast_fusion.3
  78.2 0.6 fusion.41
  78.8 0.6 bitcast_dynamic-update-slice_fusion.3
  79.4 0.2 copy.55
  79.7 0.8 dynamic-slice_bitcast_fusion.3
  80.5 0.6 fusion.41
  81.1 0.6 bitcast_dynamic-update-slice_fusion.3
  81.7 1.0 broadcast_multiply_fusion
  82.8 3.9 %mul.93 = f32[64,112,12]{2,1,0:T(8,128)} reshape(f32[8,8,1344]{2,1,0:T(8,128)S(1)} %broadcast_multiply_fusion) | data formatting | bytes 688128 | tf_op jit(solution)/shard_map/mul | solution.py:97
  86.7 2.7 %copy.38 = f32[64,112,12]{1,0,2:T(8,128)S(1)} copy(f32[64,112,12]{2,1,0:T(8,128)} %mul.93) | data formatting | bytes 688128 | tf_op jit(solution)/shard_map/mul | solution.py:97
  89.4 0.1 multiply_convert_fusion.11
  89.5 0.1 copy.39
  89.7 13.7 %all_to_all.33 = bf16[64,112,12]{1,2,0:T(8,128)(2,1)S(1)} all-to-all(bf16[64,112,12]{1,2,0:T(8,128)(2,1)S(1)} %copy.39), channel_id=1, replica_groups=mesh['member'=64,'shard'=4] {'member'}, dimensions={0} | all-to-all | bytes 344064 | tf_op jit(solution)/shard_map/all_to_all | solution.py:100
  103.4 0.1 squeeze.9
  103.5 6.1 %fusion.30 = (f32[768]{0:T(1024)S(1)}, f32[768]{0:T(1024)S(1)}, f32[768,1024]{1,0:T(8,128)}) fusion(f32[768]{0:T(1024)S(1)} %add_rsqrt_fusion, f32[768,1024]{1,0:T(8,128)} %copy-done.1, f32[768]{0:T(1024)S(1)} %broadcast_multiply_fusion.4, bf16[1024,1024]{1,0:T(8,128)(2,1)S(1)} %copy-done, f32[768,1024]{1,0:T(8,128)} %copy-done.14, ...), kind=kOutput, calls=%fused_computation.51 | convolution fusion | flops 1798568448 | bytes 11952128 | tf_op jit(solution)/shard_map/dot_general | solution.py:109
  109.7 6.2 %fusion.19 = bf16[128,1024]{1,0:T(8,128)(2,1)} fusion(f32[768,128]{1,0:T(8,128)S(1)} %copy-done.3, f32[768,1024]{1,0:T(8,128)} %get-tuple-element.56, f32[768,1024]{1,0:T(8,128)} %copy-done.1, f32[768]{0:T(1024)S(1)} %get-tuple-element.57, f32[768]{0:T(1024)S(1)} %get-tuple-element.58, f32[768]{0:T(1024)S(1)} %add_rsqrt_fusion, ...), kind=kOutput, calls=%fused_computation.28 | convolution fusion | flops 1212809216 | bytes 6959104 | tf_op jit(solution)/shard_map/dot_general | solution.py:119
  115.9 0.0 reduce-scatter.2.cloned.1.call-update
  115.9 22.9 %reduce-scatter.2.cloned.1.call-done = bf16[32,1024]{1,0:T(8,128)(2,1)} async-done(((bf16[128,1024]{1,0:T(8,128)(2,1)}), bf16[32,1024]{1,0:T(8,128)(2,1)}) %reduce-scatter.2.cloned.1.call-update) | async-done | bytes 65552 | tf_op jit(solution)/shard_map/reduce_scatter | solution.py:118
  138.8 1.5 %bitcast_convert_fusion = f32[1,32,1024]{2,1,0:T(8,128)} fusion(bf16[32,1024]{1,0:T(8,128)(2,1)} %reduce-scatter.2.cloned.1.call-done), kind=kLoop, calls=%fused_computation.40 | loop fusion | flops 32768 | bytes 196608 | tf_op jit(solution)/shard_map/broadcast_in_dim | solution.py:130
  (33 shorter events, 0.1 us)
Async XLA Ops:
  6.5 23.2 %copy-start = (bf16[1024,1024]{1,0:T(8,128)(2,1)S(1)}, bf16[1024,1024]{1,0:T(8,128)(2,1)}, u32[]{:S(2)}) copy-start(bf16[1024,1024]{1,0:T(8,128)(2,1)} %param.20) | copy-start | bytes 6291460
  27.0 0.8 copy-start.2
  29.2 2.4 %copy-start.1 = (f32[768,1024]{1,0:T(8,128)}, f32[768,1024]{1,0:T(8,128)S(1)}, u32[]{:S(2)}) copy-start(f32[768,1024]{1,0:T(8,128)S(1)} %get-tuple-element.55) | copy-start | bytes 9437188
  29.7 3.7 %copy-start.8 = (f32[1,112,768]{2,1,0:T(8,128)S(1)}, f32[1,112,768]{2,1,0:T(8,128)}, u32[]{:S(2)}) copy-start(f32[1,112,768]{2,1,0:T(8,128)} %param.16) | copy-start | bytes 1032196
  29.7 3.7 %copy-start.9 = (bf16[1024,112]{0,1:T(8,128)(2,1)S(1)}, bf16[1024,112]{0,1:T(8,128)(2,1)}, u32[]{:S(2)}) copy-start(bf16[1024,112]{0,1:T(8,128)(2,1)} %param.22) | copy-start | bytes 688132
  29.7 3.7 %copy-start.11 = (f32[1024]{0:T(1024)S(1)}, f32[1024]{0:T(1024)}, u32[]{:S(2)}) copy-start(f32[1024]{0:T(1024)} %param.21) | copy-start | bytes 12292
  29.8 3.6 %copy-start.13 = (f32[112]{0:T(128)S(1)}, f32[112]{0:T(128)}, u32[]{:S(2)}) copy-start(f32[112]{0:T(128)} %param.23) | copy-start | bytes 1348
  31.7 1.7 %copy-start.14 = (f32[768,1024]{1,0:T(8,128)}, f32[768,1024]{1,0:T(8,128)S(1)}, u32[]{:S(2)}) copy-start(f32[768,1024]{1,0:T(8,128)S(1)} %fusion.9) | copy-start | bytes 9437188
  33.4 10.7 %copy-start.5 = (f32[1,112,12]{1,0,2:T(1,128)S(1)}, f32[1,112,12]{1,0,2:T(1,128)}, u32[]{:S(2)}) copy-start(f32[1,112,12]{1,0,2:T(1,128)} %param.17) | copy-start | bytes 16132
  33.4 10.7 %copy-start.6 = (f32[112]{0:T(128)S(1)}, f32[112]{0:T(128)}, u32[]{:S(2)}) copy-start(f32[112]{0:T(128)} %param.19) | copy-start | bytes 1348
  33.4 10.7 %copy-start.7 = (f32[1,12]{1,0:T(1,128)S(1)}, f32[1,12]{1,0:T(1,128)}, u32[]{:S(2)}) copy-start(f32[1,12]{1,0:T(1,128)} %param.18) | copy-start | bytes 148
  35.5 18.0 %all-to-all-start = ((f32[1,112,768]{1,0,2:T(1,128)}), f32[1,112,768]{1,0,2:T(1,128)S(1)}, u32[]{:S(2)}, u32[]{:S(2)}) async-start(f32[1,112,768]{1,0,2:T(1,128)} %copy.34), calls=%async_computation | async-start | bytes 786432 | tf_op jit(solution)/shard_map/all_to_all | solution.py:80
  44.0 94.7 %reduce-scatter.2.cloned.1.call-start = ((), (), s32[]{:S(2)}) async-start(), calls=%async_computation.3 | async-start | bytes 327680 | tf_op jit(solution)/shard_map/reduce_scatter | solution.py:118
  82.7 6.7 %copy-start.4 = (f32[112,12]{0,1:T(8,128)S(1)}, f32[112,12]{0,1:T(8,128)}, u32[]{:S(2)}) copy-start(f32[112,12]{0,1:T(8,128)} %broadcast_multiply_fusion.1) | copy-start | bytes 16132
  86.7 16.8 %copy-start.10 = (bf16[1024,112]{0,1:T(8,128)(2,1)S(1)}, bf16[1024,112]{0,1:T(8,128)(2,1)}, u32[]{:S(2)}) copy-start(bf16[1024,112]{0,1:T(8,128)(2,1)} %param.22) | copy-start | bytes 688132
  86.7 16.8 %copy-start.12 = (f32[1024]{0:T(1024)S(1)}, f32[1024]{0:T(1024)}, u32[]{:S(2)}) copy-start(f32[1024]{0:T(1024)} %param.21) | copy-start | bytes 12292
  103.5 6.2 %copy-start.3 = (f32[768,128]{1,0:T(8,128)S(1)}, f32[768,128]{1,0:T(8,128)}, u32[]{:S(2)}) copy-start(f32[768,128]{1,0:T(8,128)} %copy-done.2) | copy-start | bytes 1179652
Sparse Core Ops, SparseCore 0:
  116.0 22.7 reduce-scatter.1
where the time goes:
time: 148 us; the launch traced here: 147 us
  local copies, waits for them, and re-layouts  34.9 us (24%)
  blocking collectives  31.8 us (21%)
  waiting for transfers between devices  31.7 us (21%)
  matrix products  16.8 us (11%)
  between operations  13.7 us (9%)
  other arithmetic  9.67 us (7%)
  starting transfers between devices  8.52 us (6%)
    reduce_scatter x1, waiting for transfers between devices, local(): lax.psum_scatter(lax.dot_general(matrix, grad_cell, (((0,), (0,)), ((), (...  22.9 us
    all_gather x1, blocking collectives, local(): shard_rows = lax.all_gather(mesh_local, 'shard', axis=0, tiled=True)  18.1 us
    all_to_all x1, blocking collectives, local(): lax.all_to_all(slopes, 'member', split_axis=0, concat_axis=2, tiled=True)[0]  13.7 us
    sub x17, local copies, waits for them, and re-layouts, group_pairs(): return jnp.sum(softened_slope(chosen[:, None] - flattened[None]), axis=1)  9.59 us
    all_to_all x1, waiting for transfers between devices, local(): lax.all_to_all(prediction_piece[None], 'member', split_axis=2, concat_axi...  8.79 us
    all_to_all x1, starting transfers between devices, local(): lax.all_to_all(prediction_piece[None], 'member', split_axis=2, concat_axi...  8.48 us
    mul x2, local copies, waits for them, and re-layouts, local(): (1.0 - fairness_factor) / (members - 1) * pairwise_sums  6.63 us
    dot_general x1, matrix products, local(): lax.dot_general(matrix, grad_cell, (((0,), (0,)), ((), ())), precision=la...  6.18 us
  transfers between devices with their start and end apart: 2, of which 2 were waited for; matrix products, arithmetic and copies ran while one was open for 0% of the time, Pallas kernels for 0%

commit v1 on v0

v1 whole, which is shorter than its diff:
```python
import jax
import jax.numpy as jnp
from jax import lax
from jax.experimental import pallas as pl
from jax.experimental.pallas import tpu as pltpu
from jax.sharding import PartitionSpec as P

smoothing = 0.05
fairness = 0.95
epsilon = 1e-05

MESH_ID = pl.DeviceIdType.MESH
F32 = jnp.float32
BF16 = jnp.bfloat16
NN = (((1,), (0,)), ((), ()))
NT = (((1,), (1,)), ((), ()))


def slope(differ):
    return differ * lax.rsqrt(differ * differ + smoothing * smoothing)


def dot(a, b, dims, precision=None):
    return lax.dot_general(a, b, dims, precision=precision, preferred_element_type=F32)


def split(value):
    high = value.astype(BF16)
    return high, (value - high.astype(F32)).astype(BF16)


def kernel(
    members,
    mesh_in,
    stencil_in,
    weight_in,
    prev_in,
    observed_in,
    area_in,
    var_in,
    hidden_in,
    hidden_bias_in,
    output_in,
    output_bias_in,
    out_ref,
    gathered,
    stencil,
    weight,
    prev,
    observed,
    area,
    var,
    hidden,
    hidden_bias,
    output,
    output_bias,
    cells_mat,
    mesh_split,
    blend,
    blend_t,
    product,
    slope_act,
    grad_side,
    target,
    coefficient,
    forecast_out,
    forecast_in,
    state,
    sums,
    cot_out,
    cot_in,
    part_out,
    part_hop,
    part_in,
    local_sem,
    gather_send,
    gather_recv,
    cast_send,
    cast_recv,
    back_send,
    back_recv,
    part_send,
    part_recv,
):
    me = lax.axis_index("member")
    spot = lax.axis_index("shard")
    right = lax.rem(spot + 1, 4)
    left = lax.rem(spot + 3, 4)
    across = lax.rem(spot + 2, 4)
    variables = 112
    chunk_rows = 192

    loads = [
        pltpu.make_async_copy(source, target_ref, local_sem.at[number])
        for number, (source, target_ref) in enumerate(
            (
                (mesh_in, gathered.at[pl.ds(2 * spot, 2)]),
                (stencil_in, stencil),
                (weight_in, weight),
                (prev_in, prev),
                (observed_in, observed),
                (area_in, area),
                (var_in, var),
                (hidden_in, hidden),
                (hidden_bias_in, hidden_bias),
                (output_in, output.at[pl.ds(0, variables)]),
                (output_bias_in, output_bias),
            )
        )
    ]
    for load in loads:
        load.start()

    barrier = pltpu.get_barrier_semaphore()

    @pl.loop(1, members)
    def _(offset):
        pl.semaphore_signal(
            barrier,
            inc=1,
            device_id={"member": lax.rem(me + offset, members)},
            device_id_type=MESH_ID,
        )

    for neighbour in (left, right):
        pl.semaphore_signal(
            barrier, inc=1, device_id={"shard": neighbour}, device_id_type=MESH_ID
        )
    pl.semaphore_wait(barrier, members + 1)

    def gather_copy(number, source, slot, to):
        return pltpu.make_async_remote_copy(
            src_ref=source,
            dst_ref=gathered.at[slot],
            send_sem=gather_send.at[number],
            recv_sem=gather_recv.at[number],
            device_id={"shard": to},
            device_id_type=MESH_ID,
        )

    own = [
        gather_copy(0, mesh_in.at[0], 2 * spot, right),
        gather_copy(1, mesh_in.at[1], 2 * spot + 1, left),
        gather_copy(2, mesh_in.at[1], 2 * spot + 1, right),
        gather_copy(3, mesh_in.at[0], 2 * spot, left),
    ]
    for copy in own:
        copy.start()

    for load in loads[1:7]:
        load.wait()
    loads[10].wait()
    row_ids = lax.broadcasted_iota(jnp.int32, (128, 768), 0)
    cells_t = jnp.zeros((128, 768), F32)
    for k in range(3):
        cells_t = cells_t + jnp.where(stencil[k] == row_ids, weight[k], 0.0)
    cells_mat[...] = cells_t.T

    own[0].wait_recv()
    relay_right = gather_copy(4, gathered.at[2 * left], 2 * left, right)
    relay_right.start()
    own[1].wait_recv()
    relay_left = gather_copy(5, gathered.at[2 * right + 1], 2 * right + 1, left)
    relay_left.start()

    slots = lax.broadcasted_iota(jnp.int32, (16, 768), 0)
    slots = jnp.where(slots < 12, slots, slots - 4)
    chosen = jnp.where(
        lax.broadcasted_iota(jnp.int32, (16, 768), 1) == slots + 12 * me, 1.0, 0.0
    ).astype(F32)
    target[...] = jnp.zeros((16, 128), F32)
    for slot in range(16):
        cell = slot if slot < 12 else slot - 4
        target[slot : slot + 1, :variables] = observed[cell] - output_bias[...]
    target[:, :variables] = target[:, :variables] - dot(
        chosen, prev[...], NT, lax.Precision.HIGHEST
    )
    lanes = lax.broadcasted_iota(jnp.int32, (16, 12), 1)
    cell_ids = lax.broadcasted_iota(jnp.int32, (16, 12), 0)
    cell_ids = jnp.where(cell_ids < 12, cell_ids, cell_ids - 4)
    area_column = jnp.sum(
        jnp.where(lanes == cell_ids, area[...], 0.0), axis=1, keepdims=True
    )
    coefficient[...] = jnp.zeros((16, 128), F32)
    coefficient[:, :variables] = area_column * var[...]
    output[variables:, :] = jnp.zeros((128 - variables, 1024), BF16)

    own[2].wait_recv()
    own[3].wait_recv()
    relay_right.wait_recv()
    relay_left.wait_recv()
    loads[0].wait()
    loads[7].wait()
    loads[8].wait()
    loads[9].wait()

    rows = gathered[...].reshape(128, 1024).astype(F32)
    rows = rows - jnp.mean(rows, axis=1, keepdims=True)
    row_high, row_low = split(rows)
    mesh_split[:128] = row_high
    mesh_split[128:] = row_low
    gram_parts = dot(mesh_split[...], mesh_split[:128], NT)
    gram = (gram_parts[:128] + gram_parts[128:] + gram_parts[128:].T) * (1.0 / 1024)
    through_parts = dot(mesh_split[...], hidden[...], NN)
    through = through_parts[:128] + through_parts[128:]
    through_high, through_low = split(through)
    through_all = jnp.concatenate([through_high, through_low, through_high], axis=0)
    cells = cells_mat[...]
    variance = jnp.sum(
        cells * dot(cells, gram, NN, lax.Precision.HIGHEST), axis=1, keepdims=True
    )
    scaled = cells * lax.rsqrt(variance + epsilon)
    cells_mat[...] = scaled
    scaled_high, scaled_low = split(scaled)
    blend[:, :128] = scaled_high
    blend[:, 128:256] = scaled_high
    blend[:, 256:] = scaled_low

    def cast_copy(to):
        return pltpu.make_async_remote_copy(
            src_ref=forecast_out.at[to],
            dst_ref=forecast_in.at[me],
            send_sem=cast_send,
            recv_sem=cast_recv,
            device_id={"member": to},
            device_id_type=MESH_ID,
        )

    @pl.loop(0, 4)
    def _(step):
        part = lax.rem(lax.div(me, 16) + step, 4)
        span = pl.ds(pl.multiple_of(part * chunk_rows, chunk_rows), chunk_rows)
        raw = dot(blend[span], through_all, NN)
        product[span] = raw
        act = raw + hidden_bias[...]
        active = act * (0.5 * jnp.tanh(0.5 * act) + 0.5)
        update = dot(active.astype(BF16), output[...], NT)
        for piece in range(48):
            forecast_out[part * 16 + piece // 3, piece % 3] = update[
                piece * 4 : piece * 4 + 4
            ]

        @pl.loop(0, 16)
        def _(offset):
            to = part * 16 + lax.rem(me + 1 + offset, 16)

            @pl.when(to != me)
            def _():
                cast_copy(to).start()

    forecast_in[me] = forecast_out[me]
    blend_t[...] = cells_mat[...].T.astype(BF16)

    @pl.loop(0, 4)
    def _(part):
        span = pl.ds(pl.multiple_of(part * chunk_rows, chunk_rows), chunk_rows)
        act = product[span] + hidden_bias[...]
        gate = 0.5 * jnp.tanh(0.5 * act) + 0.5
        slope_act[span] = gate * (1.0 + act * (1.0 - gate))

    others = pl.ds(0, members - 1)
    pltpu.make_async_copy(forecast_in.at[others], forecast_in.at[others], cast_recv).wait()

    for m in range(64):
        state[m] = jnp.concatenate([forecast_in[m, 0], forecast_in[m, 1]], axis=0)
    for m in range(32):
        state[64 + m] = jnp.concatenate([forecast_in[m, 2], forecast_in[m + 32, 2]], axis=0)

    def half_turn(value):
        return pltpu.roll(value, 4, 0)

    @pl.loop(0, 8)
    def _(block):
        base = block * 8
        values = [state[base + i] for i in range(8)]
        totals = [jnp.zeros((8, 128), F32) for _ in range(8)]
        for i in range(8):
            for j in range(i + 1, 8):
                push = slope(values[i] - values[j])
                totals[i] = totals[i] + push
                totals[j] = totals[j] - push
        for i in range(8):
            sums[base + i] = totals[i]

    @pl.loop(0, 28)
    def _(step):
        first = lax.rem(step, 8) * 8
        second = lax.rem(lax.rem(step, 8) + lax.div(step, 8) + 1, 8) * 8
        values = [state[first + i] for i in range(8)]
        totals = [sums[first + i] for i in range(8)]
        for j in range(8):
            other = state[second + j]
            total = sums[second + j]
            for i in range(8):
                push = slope(values[i] - other)
                totals[i] = totals[i] + push
                total = total - push
            sums[second + j] = total
        for i in range(8):
            sums[first + i] = totals[i]

    @pl.loop(0, 4)
    def _(block):
        base = 64 + block * 8
        values = [state[base + i] for i in range(8)]
        turned = [half_turn(value) for value in values]
        totals = [slope(values[i] - turned[i]) for i in range(8)]
        crossed = [jnp.zeros((8, 128), F32) for _ in range(8)]
        for i in range(8):
            for j in range(i + 1, 8):
                push = slope(values[i] - values[j])
                totals[i] = totals[i] + push
                totals[j] = totals[j] - push
                push = slope(values[i] - turned[j])
                totals[i] = totals[i] + push
                crossed[j] = crossed[j] - push
        for i in range(8):
            sums[base + i] = totals[i] + half_turn(crossed[i])

    @pl.loop(0, 6)
    def _(step):
        first = 64 + lax.rem(step, 4) * 8
        second = 64 + lax.rem(lax.rem(step, 4) + lax.div(step, 4) + 1, 4) * 8
        values = [state[first + i] for i in range(8)]
        totals = [sums[first + i] for i in range(8)]
        for j in range(8):
            other = state[second + j]
            turned = half_turn(other)
            total = sums[second + j]
            crossed = jnp.zeros((8, 128), F32)
            for i in range(8):
                push = slope(values[i] - other)
                totals[i] = totals[i] + push
                total = total - push
                push = slope(values[i] - turned)
                totals[i] = totals[i] + push
                crossed = crossed - push
            sums[second + j] = total + half_turn(crossed)
        for i in range(8):
            sums[first + i] = totals[i]

    pair_factor = (1.0 - (1.0 - fairness) / members) / (members - 1)

    def back_copy(to):
        return pltpu.make_async_remote_copy(
            src_ref=cot_out.at[to],
            dst_ref=cot_in.at[me],
            send_sem=back_send,
            recv_sem=back_recv,
            device_id={"member": to},
            device_id_type=MESH_ID,
        )

    @pl.loop(0, 32)
    def _(m):
        for extra in (0, 32):
            cot = coefficient[:8] * (
                slope(state[m + extra] - target[:8]) - pair_factor * sums[m + extra]
            )
            cot_out[m + extra, 0] = cot[:4].astype(BF16)
            cot_out[m + extra, 1] = cot[4:].astype(BF16)
        cot = coefficient[8:] * (
            slope(state[64 + m] - target[8:]) - pair_factor * sums[64 + m]
        )
        cot_out[m, 2] = cot[:4].astype(BF16)
        cot_out[m + 32, 2] = cot[4:].astype(BF16)

    @pl.loop(1, members)
    def _(offset):
        back_copy(lax.rem(me + offset, members)).start()

    cot_in[me] = cot_out[me]
    pltpu.make_async_copy(cot_in.at[others], cot_in.at[others], back_recv).wait()

    @pl.loop(0, 4)
    def _(part):
        span = pl.ds(pl.multiple_of(part * chunk_rows, chunk_rows), chunk_rows)
        cot = jnp.concatenate(
            [cot_in[part * 16 + piece // 3, piece % 3].astype(F32) for piece in range(48)],
            axis=0,
        ).astype(BF16)
        grad = dot(cot, output[...], NN) * slope_act[span]
        grad_side[span, :1024] = grad.astype(BF16)
        along = jnp.sum(grad * product[span], axis=1, keepdims=True) * (1.0 / 1024)
        grad_side[span, 1024:] = (cells_mat[span] * along).astype(BF16)

    joined = dot(blend_t[...], grad_side[...], NN)
    result = dot(joined[:, :1024].astype(BF16), hidden[...], NT)
    result = result - dot(joined[:, 1024:].astype(BF16), mesh_split[:128], NN)
    result = result - jnp.mean(result, axis=1, keepdims=True)
    product[:128] = result
    part_out[...] = result.astype(BF16).reshape(8, 16, 1024)

    def part_copy(number, source, slot, to):
        return pltpu.make_async_remote_copy(
            src_ref=source,
            dst_ref=part_in.at[slot],
            send_sem=part_send.at[number],
            recv_sem=part_recv.at[number],
            device_id={"shard": to},
            device_id_type=MESH_ID,
        )

    hops = [
        part_copy(0, part_out.at[2 * across], 0, right),
        part_copy(1, part_out.at[2 * across + 1], 1, left),
        part_copy(2, part_out.at[2 * right + 1], 2, right),
        part_copy(3, part_out.at[2 * left], 3, left),
    ]
    for hop in hops:
        hop.start()
    def tile(slot):
        return product[pl.ds(pl.multiple_of(slot * 16, 16), 16)]

    hops[0].wait_recv()
    part_hop[0] = (part_in[0].astype(F32) + tile(2 * right)).astype(BF16)
    hops.append(part_copy(4, part_hop.at[0], 4, right))
    hops[4].start()
    hops[1].wait_recv()
    part_hop[1] = (part_in[1].astype(F32) + tile(2 * left + 1)).astype(BF16)
    hops.append(part_copy(5, part_hop.at[1], 5, left))
    hops[5].start()
    for hop in hops[2:]:
        hop.wait_recv()
    out_ref[:16] = tile(2 * spot) + part_in[4].astype(F32) + part_in[3].astype(F32)
    out_ref[16:] = tile(2 * spot + 1) + part_in[2].astype(F32) + part_in[5].astype(F32)

    for copy in own + [relay_right, relay_left] + hops:
        copy.wait_send()
    pltpu.make_async_copy(forecast_out.at[others], forecast_out.at[others], cast_send).wait()
    pltpu.make_async_copy(cot_out.at[others], cot_out.at[others], back_send).wait()


def local(
    processor_latent,
    stencil_index,
    interp_weight,
    prev_state,
    observed,
    cell_area,
    var_weight,
    hidden_weight,
    hidden_bias,
    output_weight,
    output_bias,
):
    members = lax.axis_size("member")
    operands = (
        processor_latent.reshape(2, 16, 1024),
        jnp.transpose(stencil_index, (1, 0, 2)),
        jnp.transpose(interp_weight, (1, 0, 2)),
        prev_state[0],
        jnp.transpose(observed, (2, 0, 1)),
        cell_area,
        var_weight.reshape(1, -1),
        hidden_weight,
        hidden_bias.reshape(1, -1),
        output_weight.T,
        output_bias.reshape(1, -1),
    )

    def body(*refs):
        kernel(members, *refs)

    vmem = pltpu.VMEM
    dma = pltpu.SemaphoreType.DMA
    out = pl.pallas_call(
        body,
        name="decoder_step",
        out_shape=jax.ShapeDtypeStruct((32, 1024), F32),
        in_specs=[pl.BlockSpec(memory_space=pl.ANY)] * len(operands),
        out_specs=pl.BlockSpec(memory_space=pltpu.VMEM),
        scratch_shapes=[
            vmem((8, 16, 1024), BF16),
            vmem((3, 1, 768), jnp.int32),
            vmem((3, 1, 768), F32),
            vmem((112, 768), F32),
            vmem((12, 1, 112), F32),
            vmem((1, 12), F32),
            vmem((1, 112), F32),
            vmem((1024, 1024), BF16),
            vmem((1, 1024), F32),
            vmem((128, 1024), BF16),
            vmem((1, 112), F32),
            vmem((768, 128), F32),
            vmem((256, 1024), BF16),
            vmem((768, 384), BF16),
            vmem((128, 768), BF16),
            vmem((768, 1024), F32),
            vmem((768, 1024), F32),
            vmem((768, 1152), BF16),
            vmem((16, 128), F32),
            vmem((16, 128), F32),
            vmem((64, 3, 4, 128), F32),
            vmem((64, 3, 4, 128), F32),
            vmem((96, 8, 128), F32),
            vmem((96, 8, 128), F32),
            vmem((64, 3, 4, 128), BF16),
            vmem((64, 3, 4, 128), BF16),
            vmem((8, 16, 1024), BF16),
            vmem((2, 16, 1024), BF16),
            vmem((6, 16, 1024), BF16),
            dma((11,)),
            dma((6,)),
            dma((6,)),
            dma,
            dma,
            dma,
            dma,
            dma((6,)),
            dma((6,)),
        ],
        compiler_params=pltpu.CompilerParams(collective_id=0, has_side_effects=True),
    )(*operands)
    return out[None]


def solution(mesh):
    in_specs = (
        P("member", "shard", None),
        P("shard", None, None),
        P("shard", None, None),
        P("shard", None, None),
        P("shard", None, "member"),
        P("shard", "member"),
        P(),
        P(),
        P(),
        P(),
        P(),
    )
    out_specs = P("member", "shard", None)
    return jax.shard_map(local, mesh=mesh, in_specs=in_specs, out_specs=out_specs, check_vma=False)
```

time: 148 us -> 52.7 us (0.36)
  Pallas kernels: 0 us -> 50.7 us
  local copies, waits for them, and re-layouts: 34.9 us -> 1.57 us
  blocking collectives: 31.8 us -> 0 us
  waiting for transfers between devices: 31.7 us -> 0 us
  matrix products: 16.8 us -> 0 us
  between operations: 13.7 us -> 0.01 us
  other arithmetic: 9.67 us -> 0 us
  starting transfers between devices: 8.52 us -> 0 us
    pallas_call x0 -> x1, Pallas kernels: none -> 50.7 us  [local(): pl.pallas_call(body, name='decoder_step', out_shape=jax.ShapeDtypeStruct(...]
    reduce_scatter x1 -> x0, waiting for transfers between devices: 22.9 us -> none  [local(): lax.psum_scatter(lax.dot_general(matrix, grad_cell, (((0,), (0,)), ((), (...]
    all_gather x1 -> x0, blocking collectives: 18.1 us -> none  [local(): shard_rows = lax.all_gather(mesh_local, 'shard', axis=0, tiled=True)]
    dot_general x5 -> x0, matrix products: 16.8 us -> none  [the longest x1 6.18 us: local(): lax.dot_general(matrix, grad_cell, (((0,), (0,)), ((), ())), precision=la...]
    all_to_all x1 -> x0, blocking collectives: 13.7 us -> none  [local(): lax.all_to_all(slopes, 'member', split_axis=0, concat_axis=2, tiled=True)[0]]
    sub x17 -> x0, local copies, waits for them, and re-layouts: 9.59 us -> none  [group_pairs(): return jnp.sum(softened_slope(chosen[:, None] - flattened[None]), axis=1)]
    all_to_all x1 -> x0, waiting for transfers between devices: 8.79 us -> none  [local(): lax.all_to_all(prediction_piece[None], 'member', split_axis=2, concat_axi...]
    all_to_all x1 -> x0, starting transfers between devices: 8.48 us -> none  [local(): lax.all_to_all(prediction_piece[None], 'member', split_axis=2, concat_axi...]
  transfers between devices with their start and end apart: 2 -> 0, of which waited for: 2 -> 0; matrix products, arithmetic and copies ran while one was open for 0% -> 0% of each run, Pallas kernels for 0% -> 0%
where the time goes in v1:
time: 52.7 us; the launch traced here: 52.3 us
  Pallas kernels  50.7 us (96%)
  local copies, waits for them, and re-layouts  1.57 us (3%)
    pallas_call x1, Pallas kernels, local(): pl.pallas_call(body, name='decoder_step', out_shape=jax.ShapeDtypeStruct(...  50.7 us
    unnamed x1, local copies, waits for them, and re-layouts  1.57 us

profile of v1, /device:TPU:2, one launch (start us, length us, event | category | flops | bytes accessed | tf_op | source)
XLA Modules:
  0.0 52.3 jit_solution(7220206130944380870)
XLA Ops:
  0.0 50.7 %decoder_step.1 = f32[32,1024]{1,0:T(8,128)} custom-call(bf16[2,16,1024]{2,1,0:T(8,128)(2,1)} %bitcast.13, s32[3,1,768]{2,1,0:T(1,128)} %bitcast.14, f32[3,1,768]{2,1,0:T(1,128)} %bitcast.15, f32[112,768]{1,0:T(8,128)} %bitcast.11, f32[12,1,112]{2,1,0:T(1,128)} %bitcast.16, f32[1,12]{1,0:T(1,128)} %refs_5_.1, f32[1,112]{1,0:T(1,128)} %bitcast.18, ...), custom_call_target="tpu_custom_call" | custom-call | tf_op jit(solution)/shard_map/decoder_step/pallas_call | solution.py:467
  50.7 1.6 %copy.13 = f32[1,32,1024]{2,1,0:T(8,128)} copy(f32[1,32,1024]{2,1,0:T(8,128)} %bitcast.10) | data formatting | bytes 262144

commit v2 on v1

v2 whole, which is shorter than its diff:
```python
import jax
import jax.numpy as jnp
from jax import lax
from jax.experimental import pallas as pl
from jax.experimental.pallas import tpu as pltpu
from jax.sharding import PartitionSpec as P

smoothing = 0.05
fairness = 0.95
epsilon = 1e-05

MESH_ID = pl.DeviceIdType.MESH
F32 = jnp.float32
BF16 = jnp.bfloat16
NN = (((1,), (0,)), ((), ()))
NT = (((1,), (1,)), ((), ()))
VARS = 112


def slope(differ):
    return differ * lax.rsqrt(differ * differ + smoothing * smoothing)


def dot(a, b, dims, precision=None):
    return lax.dot_general(a, b, dims, precision=precision, preferred_element_type=F32)


def split(value):
    high = value.astype(BF16)
    return high, (value - high.astype(F32)).astype(BF16)


def ring():
    spot = lax.axis_index("shard")
    return spot, lax.rem(spot + 1, 4), lax.rem(spot + 3, 4), lax.rem(spot + 2, 4)


def signal(barrier, axis, to):
    pl.semaphore_signal(barrier, inc=1, device_id={axis: to}, device_id_type=MESH_ID)


def gather_kernel(
    mesh_in,
    stencil_in,
    weight_in,
    prev_in,
    observed_in,
    area_in,
    var_in,
    output_bias_in,
    hidden_in,
    hidden_bias_in,
    output_in,
    gathered,
    cells_ref,
    target,
    coefficient,
    hidden,
    hidden_bias,
    output,
    stencil,
    weight,
    prev,
    observed,
    area,
    var,
    output_bias,
    local_sem,
    send_sem,
    recv_sem,
):
    me = lax.axis_index("member")
    spot, right, left, _ = ring()
    barrier = pltpu.get_barrier_semaphore()
    for neighbour in (left, right):
        signal(barrier, "shard", neighbour)
    loads = [
        pltpu.make_async_copy(source, place, local_sem.at[number])
        for number, (source, place) in enumerate(
            (
                (stencil_in, stencil),
                (weight_in, weight),
                (prev_in, prev),
                (observed_in, observed),
                (area_in, area),
                (var_in, var),
                (output_bias_in, output_bias),
                (mesh_in, gathered.at[pl.ds(2 * spot, 2)]),
                (hidden_in, hidden),
                (hidden_bias_in, hidden_bias),
                (output_in, output.at[pl.ds(0, VARS)]),
            )
        )
    ]
    for load in loads:
        load.start()
    pl.semaphore_wait(barrier, 2)

    def copy(number, source, slot, to):
        return pltpu.make_async_remote_copy(
            src_ref=source,
            dst_ref=gathered.at[slot],
            send_sem=send_sem.at[number],
            recv_sem=recv_sem.at[number],
            device_id={"shard": to},
            device_id_type=MESH_ID,
        )

    own = [
        copy(0, mesh_in.at[0], 2 * spot, right),
        copy(1, mesh_in.at[1], 2 * spot + 1, left),
        copy(2, mesh_in.at[1], 2 * spot + 1, right),
        copy(3, mesh_in.at[0], 2 * spot, left),
    ]
    for each in own:
        each.start()
    for load in loads[:7]:
        load.wait()

    row_ids = lax.broadcasted_iota(jnp.int32, (128, 768), 0)
    cells_t = jnp.zeros((128, 768), F32)
    for k in range(3):
        cells_t = cells_t + jnp.where(stencil[k] == row_ids, weight[k], 0.0)
    natural = lax.broadcasted_iota(jnp.int32, (768, 768), 1)
    place = lax.broadcasted_iota(jnp.int32, (768, 768), 0)
    cell_of = jnp.where(
        place < 512,
        lax.shift_right_logical(place, 3) * 12 + (place & 7),
        lax.shift_right_logical(place - 512, 2) * 12 + 8 + (place & 3),
    )
    order = jnp.where(natural == cell_of, 1.0, 0.0).astype(BF16)
    high, rest = split(cells_t)
    middle = (cells_t - high.astype(F32)) - rest.astype(F32)
    cells_ref[...] = (
        dot(order, high, NT) + dot(order, rest, NT) + dot(order, middle.astype(BF16), NT)
    )

    slots = lax.broadcasted_iota(jnp.int32, (16, 768), 0)
    slots = jnp.where(slots < 12, slots, slots - 4)
    chosen = jnp.where(
        lax.broadcasted_iota(jnp.int32, (16, 768), 1) == slots + 12 * me, 1.0, 0.0
    ).astype(F32)
    target[...] = jnp.zeros((16, 128), F32)
    for slot in range(16):
        cell = slot if slot < 12 else slot - 4
        target[slot : slot + 1, :VARS] = observed[cell] - output_bias[...]
    target[:, :VARS] = target[:, :VARS] - dot(chosen, prev[...], NT, lax.Precision.HIGHEST)
    lanes = lax.broadcasted_iota(jnp.int32, (16, 12), 1)
    cell_ids = lax.broadcasted_iota(jnp.int32, (16, 12), 0)
    cell_ids = jnp.where(cell_ids < 12, cell_ids, cell_ids - 4)
    area_column = jnp.sum(
        jnp.where(lanes == cell_ids, area[...], 0.0), axis=1, keepdims=True
    )
    coefficient[...] = jnp.zeros((16, 128), F32)
    coefficient[:, :VARS] = area_column * var[...]

    own[0].wait_recv()
    relay_right = copy(4, gathered.at[2 * left], 2 * left, right)
    relay_right.start()
    own[1].wait_recv()
    relay_left = copy(5, gathered.at[2 * right + 1], 2 * right + 1, left)
    relay_left.start()
    output[VARS:] = jnp.zeros((128 - VARS, 1024), BF16)
    for load in loads[7:]:
        load.wait()
    for each in own[2:] + [relay_right, relay_left]:
        each.wait_recv()
    for each in own + [relay_right, relay_left]:
        each.wait_send()


def score_kernel(
    members,
    gathered,
    cells_ref,
    target,
    coefficient,
    hidden,
    hidden_bias,
    output,
    out_ref,
    blend,
    blend_t,
    product,
    slope_act,
    grad_side,
    joined,
    forecast_out_a,
    forecast_out_b,
    forecast_in_a,
    forecast_in_b,
    state_b,
    sums_a,
    sums_b,
    cot_out_a,
    cot_out_b,
    cot_in_a,
    cot_in_b,
    result_ref,
    part_out,
    part_hop,
    part_in,
    cast_send,
    cast_recv,
    back_send,
    back_recv,
    part_send,
    part_recv,
):
    me = lax.axis_index("member")
    spot, right, left, across = ring()
    barrier = pltpu.get_barrier_semaphore()

    @pl.loop(1, members)
    def _(offset):
        signal(barrier, "member", lax.rem(me + offset, members))

    for neighbour in (left, right):
        signal(barrier, "shard", neighbour)

    rows_low = gathered[...].reshape(128, 1024)
    rows = rows_low.astype(F32)
    average = jnp.mean(rows, axis=1, keepdims=True)
    row_high, row_low = split(rows - average)
    cross = dot(row_low, row_high, NT)
    gram = (dot(row_high, row_high, NT) + cross + cross.T) * (1.0 / 1024)
    through_all = dot(
        jnp.concatenate([rows_low, jnp.ones((16, 1024), BF16)], axis=0), hidden[...], NN
    )
    through = through_all[:128] - average * through_all[128:129]
    through_high, through_low = split(through)
    stack = jnp.concatenate([through_high, through_low, through_high], axis=0)
    cells = cells_ref[...]
    variance = jnp.sum(
        cells * dot(cells, gram, NN, lax.Precision.HIGHEST), axis=1, keepdims=True
    )
    scaled = cells * lax.rsqrt(variance + epsilon)
    scaled_high, scaled_low = split(scaled)
    blend[:, :128] = scaled_high
    blend[:, 128:256] = scaled_high
    blend[:, 256:] = scaled_low

    def exchange(source, place, to, send, recv):
        return pltpu.make_async_remote_copy(
            src_ref=source.at[to],
            dst_ref=place.at[me],
            send_sem=send,
            recv_sem=recv,
            device_id={"member": to},
            device_id_type=MESH_ID,
        )

    def send_forecast(source, place, number, first, count):
        @pl.loop(0, count)
        def _(offset):
            to = first + lax.rem(me + 1 + offset, count)

            @pl.when(to != me)
            def _():
                exchange(source, place, to, cast_send.at[number], cast_recv.at[number]).start()

    def updates(span):
        raw = dot(blend[span], stack, NN)
        product[span] = raw
        act = raw + hidden_bias[...]
        active = act * (0.5 * jnp.tanh(0.5 * act) + 0.5)
        return dot(active.astype(BF16), output[...], NT)

    pl.semaphore_wait(barrier, members + 1)

    @pl.loop(0, 4)
    def _(step):
        part = lax.rem(lax.div(me, 16) + 1 + step, 4)
        update = updates(pl.ds(pl.multiple_of(part * 128, 128), 128))
        forecast_out_a[pl.ds(part * 16, 16)] = update.reshape(16, 8, 128)
        send_forecast(forecast_out_a, forecast_in_a, 0, part * 16, 16)

    @pl.loop(0, 2)
    def _(step):
        part = lax.rem(lax.div(me, 32) + 1 + step, 2)
        update = updates(pl.ds(pl.multiple_of(512 + part * 128, 128), 128))
        for piece in range(32):
            forecast_out_b[part * 32 + piece] = update[piece * 4 : piece * 4 + 4]
        send_forecast(forecast_out_b, forecast_in_b, 1, part * 32, 32)

    forecast_in_a[me] = forecast_out_a[me]
    forecast_in_b[me] = forecast_out_b[me]
    blend_t[...] = blend[:, :128].astype(F32).T.astype(BF16)

    @pl.loop(0, 6)
    def _(part):
        span = pl.ds(pl.multiple_of(part * 128, 128), 128)
        act = product[span] + hidden_bias[...]
        gate = 0.5 * jnp.tanh(0.5 * act) + 0.5
        slope_act[span] = gate * (1.0 + act * (1.0 - gate))

    others = pl.ds(0, members - 1)

    def settle(ref, sem):
        pltpu.make_async_copy(ref.at[others], ref.at[others], sem).wait()

    settle(forecast_in_a, cast_recv.at[0])

    @pl.loop(0, 8)
    def _(block):
        base = block * 8
        values = [forecast_in_a[base + i] for i in range(8)]
        totals = [jnp.zeros((8, 128), F32) for _ in range(8)]
        for i in range(8):
            for j in range(i + 1, 8):
                push = slope(values[i] - values[j])
                totals[i] = totals[i] + push
                totals[j] = totals[j] - push
        for i in range(8):
            sums_a[base + i] = totals[i]

    @pl.loop(0, 28)
    def _(step):
        first = lax.rem(step, 8) * 8
        second = lax.rem(lax.rem(step, 8) + lax.div(step, 8) + 1, 8) * 8
        values = [forecast_in_a[first + i] for i in range(8)]
        totals = [sums_a[first + i] for i in range(8)]
        for j in range(8):
            other = forecast_in_a[second + j]
            total = sums_a[second + j]
            for i in range(8):
                push = slope(values[i] - other)
                totals[i] = totals[i] + push
                total = total - push
            sums_a[second + j] = total
        for i in range(8):
            sums_a[first + i] = totals[i]

    pair_factor = (1.0 - (1.0 - fairness) / members) / (members - 1)

    @pl.loop(0, 8)
    def _(block):
        for i in range(8):
            m = block * 8 + i
            cot_out_a[m] = (
                coefficient[:8]
                * (slope(forecast_in_a[m] - target[:8]) - pair_factor * sums_a[m])
            ).astype(BF16)

    def send_back(source, place, number):
        @pl.loop(1, members)
        def _(offset):
            to = lax.rem(me + offset, members)
            exchange(source, place, to, back_send.at[number], back_recv.at[number]).start()

    send_back(cot_out_a, cot_in_a, 0)
    cot_in_a[me] = cot_out_a[me]

    settle(forecast_in_b, cast_recv.at[1])
    for m in range(32):
        state_b[m] = jnp.concatenate([forecast_in_b[m], forecast_in_b[m + 32]], axis=0)

    def half_turn(value):
        return pltpu.roll(value, 4, 0)

    @pl.loop(0, 4)
    def _(block):
        base = block * 8
        values = [state_b[base + i] for i in range(8)]
        turned = [half_turn(value) for value in values]
        totals = [slope(values[i] - turned[i]) for i in range(8)]
        crossed = [jnp.zeros((8, 128), F32) for _ in range(8)]
        for i in range(8):
            for j in range(i + 1, 8):
                push = slope(values[i] - values[j])
                totals[i] = totals[i] + push
                totals[j] = totals[j] - push
                push = slope(values[i] - turned[j])
                totals[i] = totals[i] + push
                crossed[j] = crossed[j] - push
        for i in range(8):
            sums_b[base + i] = totals[i] + half_turn(crossed[i])

    @pl.loop(0, 6)
    def _(step):
        first = lax.rem(step, 4) * 8
        second = lax.rem(lax.rem(step, 4) + lax.div(step, 4) + 1, 4) * 8
        values = [state_b[first + i] for i in range(8)]
        totals = [sums_b[first + i] for i in range(8)]
        for j in range(8):
            other = state_b[second + j]
            turned = half_turn(other)
            total = sums_b[second + j]
            crossed = jnp.zeros((8, 128), F32)
            for i in range(8):
                push = slope(values[i] - other)
                totals[i] = totals[i] + push
                total = total - push
                push = slope(values[i] - turned)
                totals[i] = totals[i] + push
                crossed = crossed - push
            sums_b[second + j] = total + half_turn(crossed)
        for i in range(8):
            sums_b[first + i] = totals[i]

    @pl.loop(0, 8)
    def _(block):
        for i in range(4):
            m = block * 4 + i
            cot = coefficient[8:] * (
                slope(state_b[m] - target[8:]) - pair_factor * sums_b[m]
            )
            cot_out_b[m] = cot[:4].astype(BF16)
            cot_out_b[m + 32] = cot[4:].astype(BF16)

    send_back(cot_out_b, cot_in_b, 1)
    cot_in_b[me] = cot_out_b[me]

    def backward(cot, span):
        grad = dot(cot, output[...], NN) * slope_act[span]
        grad_side[span, :1024] = grad.astype(BF16)
        along = jnp.sum(grad * product[span], axis=1, keepdims=True) * (1.0 / 1024)
        grad_side[span, 1024:] = (blend[span, :128].astype(F32) * along).astype(BF16)

    settle(cot_in_a, back_recv.at[0])

    @pl.loop(0, 4)
    def _(part):
        cot = cot_in_a[pl.ds(part * 16, 16)].astype(F32).reshape(128, 128).astype(BF16)
        backward(cot, pl.ds(pl.multiple_of(part * 128, 128), 128))

    joined[...] = dot(blend_t[:, :512], grad_side[:512], NN)
    settle(cot_in_b, back_recv.at[1])

    @pl.loop(0, 2)
    def _(part):
        cot = jnp.concatenate(
            [cot_in_b[part * 32 + piece].astype(F32) for piece in range(32)], axis=0
        ).astype(BF16)
        backward(cot, pl.ds(pl.multiple_of(512 + part * 128, 128), 128))

    total = joined[...] + dot(blend_t[:, 512:], grad_side[512:], NN)
    outer = total[:, :1024].astype(BF16)
    inner = total[:, 1024:].astype(BF16)
    result = dot(outer, hidden[...], NT)
    result = result - dot(inner, gathered[...].reshape(128, 1024), NN)
    result = result - jnp.mean(result, axis=1, keepdims=True)
    result_ref[...] = result.reshape(8, 16, 1024)
    part_out[...] = result.astype(BF16).reshape(8, 16, 1024)

    def part_copy(number, source, to):
        return pltpu.make_async_remote_copy(
            src_ref=source,
            dst_ref=part_in.at[number],
            send_sem=part_send.at[number],
            recv_sem=part_recv.at[number],
            device_id={"shard": to},
            device_id_type=MESH_ID,
        )

    hops = [
        part_copy(0, part_out.at[2 * across], right),
        part_copy(1, part_out.at[2 * across + 1], left),
        part_copy(2, part_out.at[2 * right + 1], right),
        part_copy(3, part_out.at[2 * left], left),
        part_copy(4, part_hop.at[0], right),
        part_copy(5, part_hop.at[1], left),
    ]
    for hop in hops[:4]:
        hop.start()
    hops[0].wait_recv()
    part_hop[0] = (part_in[0].astype(F32) + result_ref[2 * right]).astype(BF16)
    hops[4].start()
    hops[1].wait_recv()
    part_hop[1] = (part_in[1].astype(F32) + result_ref[2 * left + 1]).astype(BF16)
    hops[5].start()
    for hop in hops[2:]:
        hop.wait_recv()
    out_ref[:16] = result_ref[2 * spot] + part_in[4].astype(F32) + part_in[3].astype(F32)
    out_ref[16:] = result_ref[2 * spot + 1] + part_in[2].astype(F32) + part_in[5].astype(F32)

    for hop in hops:
        hop.wait_send()
    settle(forecast_out_a, cast_send.at[0])
    settle(forecast_out_b, cast_send.at[1])
    settle(cot_out_a, back_send.at[0])
    settle(cot_out_b, back_send.at[1])


def local(
    processor_latent,
    stencil_index,
    interp_weight,
    prev_state,
    observed,
    cell_area,
    var_weight,
    hidden_weight,
    hidden_bias,
    output_weight,
    output_bias,
):
    members = lax.axis_size("member")
    vmem = pltpu.VMEM
    dma = pltpu.SemaphoreType.DMA
    outside = pl.BlockSpec(memory_space=pltpu.MemorySpace.HBM)
    inside = pl.BlockSpec(memory_space=pltpu.VMEM)
    staged = pl.pallas_call(
        gather_kernel,
        name="gather_rows",
        out_shape=(
            jax.ShapeDtypeStruct((8, 16, 1024), BF16),
            jax.ShapeDtypeStruct((768, 128), F32),
            jax.ShapeDtypeStruct((16, 128), F32),
            jax.ShapeDtypeStruct((16, 128), F32),
            jax.ShapeDtypeStruct((1024, 1024), BF16),
            jax.ShapeDtypeStruct((1, 1024), F32),
            jax.ShapeDtypeStruct((128, 1024), BF16),
        ),
        in_specs=[outside] * 11,
        out_specs=(inside,) * 7,
        scratch_shapes=[
            vmem((3, 1, 768), jnp.int32),
            vmem((3, 1, 768), F32),
            vmem((112, 768), F32),
            vmem((12, 1, 112), F32),
            vmem((1, 12), F32),
            vmem((1, 112), F32),
            vmem((1, 112), F32),
            dma((11,)),
            dma((6,)),
            dma((6,)),
        ],
        compiler_params=pltpu.CompilerParams(
            collective_id=0, has_side_effects=True, vmem_limit_bytes=16 << 20
        ),
    )(
        *(
            pltpu.with_memory_space_constraint(each, pltpu.MemorySpace.HBM)
            for each in (
                processor_latent.reshape(2, 16, 1024),
                jnp.transpose(stencil_index, (1, 0, 2)),
                jnp.transpose(interp_weight, (1, 0, 2)),
                prev_state[0],
                jnp.transpose(observed, (2, 0, 1)),
                cell_area,
                var_weight.reshape(1, -1),
                output_bias.reshape(1, -1),
                hidden_weight,
                hidden_bias.reshape(1, -1),
                output_weight.T,
            )
        )
    )

    def body(*refs):
        score_kernel(members, *refs)

    out = pl.pallas_call(
        body,
        name="score_step",
        out_shape=jax.ShapeDtypeStruct((32, 1024), F32),
        in_specs=[inside] * 7,
        out_specs=inside,
        scratch_shapes=[
            vmem((768, 384), BF16),
            vmem((128, 768), BF16),
            vmem((768, 1024), F32),
            vmem((768, 1024), F32),
            vmem((768, 1152), BF16),
            vmem((128, 1152), F32),
            vmem((64, 8, 128), F32),
            vmem((64, 4, 128), F32),
            vmem((64, 8, 128), F32),
            vmem((64, 4, 128), F32),
            vmem((32, 8, 128), F32),
            vmem((64, 8, 128), F32),
            vmem((32, 8, 128), F32),
            vmem((64, 8, 128), BF16),
            vmem((64, 4, 128), BF16),
            vmem((64, 8, 128), BF16),
            vmem((64, 4, 128), BF16),
            vmem((8, 16, 1024), F32),
            vmem((8, 16, 1024), BF16),
            vmem((2, 16, 1024), BF16),
            vmem((6, 16, 1024), BF16),
            dma((2,)),
            dma((2,)),
            dma((2,)),
            dma((2,)),
            dma((6,)),
            dma((6,)),
        ],
        compiler_params=pltpu.CompilerParams(
            collective_id=1, has_side_effects=True, vmem_limit_bytes=28 << 20
        ),
    )(*staged)
    return out[None]


def solution(mesh):
    in_specs = (
        P("member", "shard", None),
        P("shard", None, None),
        P("shard", None, None),
        P("shard", None, None),
        P("shard", None, "member"),
        P("shard", "member"),
        P(),
        P(),
        P(),
        P(),
        P(),
    )
    out_specs = P("member", "shard", None)
    return jax.shard_map(local, mesh=mesh, in_specs=in_specs, out_specs=out_specs, check_vma=False)
```

time: 52.7 us -> 50.1 us (0.951)
  Pallas kernels: 50.7 us -> 48.8 us
  local copies, waits for them, and re-layouts: 1.57 us -> 0.66 us
    pallas_call x1 -> x2, Pallas kernels: 50.7 us -> 48.8 us  [the longest x1 34.5 us: local(): pl.pallas_call(body, name='score_step', out_shape=jax.ShapeDtypeStruct((3...]
    unnamed x1, local copies, waits for them, and re-layouts: 1.57 us -> 0.66 us
where the time goes in v2:
time: 50.1 us; the launch traced here: 49.5 us
  Pallas kernels  48.8 us (97%)
  local copies, waits for them, and re-layouts  0.66 us (1%)
    pallas_call x1, Pallas kernels, local(): pl.pallas_call(body, name='score_step', out_shape=jax.ShapeDtypeStruct((3...  34.5 us
    pallas_call x1, Pallas kernels, local(): pl.pallas_call(gather_kernel, name='gather_rows', out_shape=(jax.ShapeDty...  14.4 us

profile of v2, /device:TPU:2, one launch (start us, length us, event | category | flops | bytes accessed | tf_op | source)
XLA Modules:
  0.0 49.5 jit_solution(6525157119551428322)
XLA Ops:
  0.0 14.4 %gather_rows.1 = (bf16[8,16,1024]{2,1,0:T(8,128)(2,1)S(1)}, f32[768,128]{1,0:T(8,128)S(1)}, f32[16,128]{1,0:T(8,128)S(1)}, f32[16,128]{1,0:T(8,128)S(1)}, bf16[1...) custom-call(bf16[2,16,1024]{2,1,0:T(8,128)(2,1)} %bitcast.13, ...), custom_call_target="tpu_custom_call" | custom-call | tf_op jit(solution)/shard_map/gather_rows/pallas_call | solution.py:503
  14.4 34.5 %score_step.1 = f32[32,1024]{1,0:T(8,128)S(1)} custom-call(bf16[8,16,1024]{2,1,0:T(8,128)(2,1)S(1)} %get-tuple-element.12.refs_0_, f32[768,128]{1,0:T(8,128)S(1)} %get-tuple-element.13.refs_1_, f32[16,128]{1,0:T(8,128)S(1)} %get-tuple-element.14.refs_2_, f32[16,128]{1,0:T(8,128)S(1)} %get-tuple-element.15.refs_3_, ...), custom_call_target="tpu_custom_call" | custom-call | tf_op jit(solution)/shard_map/score_step/pallas_call | solution.py:554
  48.9 0.7 %copy.13 = f32[1,32,1024]{2,1,0:T(8,128)} copy(f32[1,32,1024]{2,1,0:T(8,128)S(1)} %bitcast.10) | data formatting | bytes 262144

commit v3 on v2

--- a/solution.py
+++ b/solution.py
@@ -39,7 +39,18 @@
     pl.semaphore_signal(barrier, inc=1, device_id={axis: to}, device_id_type=MESH_ID)
 
 
-def gather_kernel(
+def member_lines(me):
+    core = lax.rem(me, 2)
+    y = lax.rem(lax.div(me, 2), 4)
+    x = lax.rem(lax.div(me, 8), 4)
+    z = lax.div(me, 32)
+    x_line = [me + 8 * (lax.rem(x + step, 4) - x) for step in (1, 2, 3)]
+    y_line = [me + 2 * (lax.rem(y + step, 4) - y) for step in (1, 2, 3)]
+    return x_line, y_line, [me + 32 * (1 - 2 * z)], [me + 1 - 2 * core]
+
+
+def step_kernel(
+    members,
     mesh_in,
     stencil_in,
     weight_in,
@@ -47,17 +58,12 @@
     observed_in,
     area_in,
     var_in,
-    output_bias_in,
     hidden_in,
     hidden_bias_in,
     output_in,
+    output_bias_in,
+    out_ref,
     gathered,
-    cells_ref,
-    target,
-    coefficient,
-    hidden,
-    hidden_bias,
-    output,
     stencil,
     weight,
     prev,
@@ -65,120 +71,12 @@
     area,
     var,
     output_bias,
-    local_sem,
-    send_sem,
-    recv_sem,
-):
-    me = lax.axis_index("member")
-    spot, right, left, _ = ring()
-    barrier = pltpu.get_barrier_semaphore()
-    for neighbour in (left, right):
-        signal(barrier, "shard", neighbour)
-    loads = [
-        pltpu.make_async_copy(source, place, local_sem.at[number])
-        for number, (source, place) in enumerate(
-            (
-                (stencil_in, stencil),
-                (weight_in, weight),
-                (prev_in, prev),
-                (observed_in, observed),
-                (area_in, area),
-                (var_in, var),
-                (output_bias_in, output_bias),
-                (mesh_in, gathered.at[pl.ds(2 * spot, 2)]),
-                (hidden_in, hidden),
-                (hidden_bias_in, hidden_bias),
-                (output_in, output.at[pl.ds(0, VARS)]),
-            )
-        )
-    ]
-    for load in loads:
-        load.start()
-    pl.semaphore_wait(barrier, 2)
-
-    def copy(number, source, slot, to):
-        return pltpu.make_async_remote_copy(
-            src_ref=source,
-            dst_ref=gathered.at[slot],
-            send_sem=send_sem.at[number],
-            recv_sem=recv_sem.at[number],
-            device_id={"shard": to},
-            device_id_type=MESH_ID,
-        )
-
-    own = [
-        copy(0, mesh_in.at[0], 2 * spot, right),
-        copy(1, mesh_in.at[1], 2 * spot + 1, left),
-        copy(2, mesh_in.at[1], 2 * spot + 1, right),
-        copy(3, mesh_in.at[0], 2 * spot, left),
-    ]
-    for each in own:
-        each.start()
-    for load in loads[:7]:
-        load.wait()
-
-    row_ids = lax.broadcasted_iota(jnp.int32, (128, 768), 0)
-    cells_t = jnp.zeros((128, 768), F32)
-    for k in range(3):
-        cells_t = cells_t + jnp.where(stencil[k] == row_ids, weight[k], 0.0)
-    natural = lax.broadcasted_iota(jnp.int32, (768, 768), 1)
-    place = lax.broadcasted_iota(jnp.int32, (768, 768), 0)
-    cell_of = jnp.where(
-        place < 512,
-        lax.shift_right_logical(place, 3) * 12 + (place & 7),
-        lax.shift_right_logical(place - 512, 2) * 12 + 8 + (place & 3),
-    )
-    order = jnp.where(natural == cell_of, 1.0, 0.0).astype(BF16)
-    high, rest = split(cells_t)
-    middle = (cells_t - high.astype(F32)) - rest.astype(F32)
-    cells_ref[...] = (
-        dot(order, high, NT) + dot(order, rest, NT) + dot(order, middle.astype(BF16), NT)
-    )
-
-    slots = lax.broadcasted_iota(jnp.int32, (16, 768), 0)
-    slots = jnp.where(slots < 12, slots, slots - 4)
-    chosen = jnp.where(
-        lax.broadcasted_iota(jnp.int32, (16, 768), 1) == slots + 12 * me, 1.0, 0.0
-    ).astype(F32)
-    target[...] = jnp.zeros((16, 128), F32)
-    for slot in range(16):
-        cell = slot if slot < 12 else slot - 4
-        target[slot : slot + 1, :VARS] = observed[cell] - output_bias[...]
-    target[:, :VARS] = target[:, :VARS] - dot(chosen, prev[...], NT, lax.Precision.HIGHEST)
-    lanes = lax.broadcasted_iota(jnp.int32, (16, 12), 1)
-    cell_ids = lax.broadcasted_iota(jnp.int32, (16, 12), 0)
-    cell_ids = jnp.where(cell_ids < 12, cell_ids, cell_ids - 4)
-    area_column = jnp.sum(
-        jnp.where(lanes == cell_ids, area[...], 0.0), axis=1, keepdims=True
-    )
-    coefficient[...] = jnp.zeros((16, 128), F32)
-    coefficient[:, :VARS] = area_column * var[...]
-
-    own[0].wait_recv()
-    relay_right = copy(4, gathered.at[2 * left], 2 * left, right)
-    relay_right.start()
-    own[1].wait_recv()
-    relay_left = copy(5, gathered.at[2 * right + 1], 2 * right + 1, left)
-    relay_left.start()
-    output[VARS:] = jnp.zeros((128 - VARS, 1024), BF16)
-    for load in loads[7:]:
-        load.wait()
-    for each in own[2:] + [relay_right, relay_left]:
-        each.wait_recv()
-    for each in own + [relay_right, relay_left]:
-        each.wait_send()
-
-
-def score_kernel(
-    members,
-    gathered,
-    cells_ref,
-    target,
-    coefficient,
     hidden,
     hidden_bias,
     output,
-    out_ref,
+    cells_mat,
+    target,
+    coefficient,
     blend,
     blend_t,
     product,
@@ -200,6 +98,10 @@
     part_out,
     part_hop,
     part_in,
+    local_sem,
+    known,
+    gather_send,
+    gather_recv,
     cast_send,
     cast_recv,
     back_send,
@@ -209,14 +111,112 @@
 ):
     me = lax.axis_index("member")
     spot, right, left, across = ring()
+    lines = member_lines(me)
     barrier = pltpu.get_barrier_semaphore()
-
-    @pl.loop(1, members)
-    def _(offset):
-        signal(barrier, "member", lax.rem(me + offset, members))
-
     for neighbour in (left, right):
         signal(barrier, "shard", neighbour)
+    for line in lines:
+        for peer in line:
+            signal(barrier, "member", peer)
+    loads = [
+        pltpu.make_async_copy(source, place, local_sem.at[number])
+        for number, (source, place) in enumerate(
+            (
+                (stencil_in, stencil),
+                (weight_in, weight),
+                (prev_in, prev),
+                (observed_in, observed),
+                (area_in, area),
+                (var_in, var),
+                (output_bias_in, output_bias),
+                (mesh_in, gathered.at[pl.ds(2 * spot, 2)]),
+                (hidden_in, hidden),
+                (hidden_bias_in, hidden_bias),
+                (output_in, output.at[pl.ds(0, VARS)]),
+            )
+        )
+    ]
+    for load in loads:
+        load.start()
+    pl.semaphore_wait(barrier, 10)
+    for peer in lines[0]:
+        signal(known.at[0], "member", peer)
+
+    def copy(number, source, slot, to):
+        return pltpu.make_async_remote_copy(
+            src_ref=source,
+            dst_ref=gathered.at[slot],
+            send_sem=gather_send.at[number],
+            recv_sem=gather_recv.at[number],
+            device_id={"shard": to},
+            device_id_type=MESH_ID,
+        )
+
+    own = [
+        copy(0, mesh_in.at[0], 2 * spot, right),
+        copy(1, mesh_in.at[1], 2 * spot + 1, left),
+        copy(2, mesh_in.at[1], 2 * spot + 1, right),
+        copy(3, mesh_in.at[0], 2 * spot, left),
+    ]
+    for each in own:
+        each.start()
+    for load in loads[:7]:
+        load.wait()
+
+    row_ids = lax.broadcasted_iota(jnp.int32, (128, 768), 0)
+    cells_t = jnp.zeros((128, 768), F32)
+    for k in range(3):
+        cells_t = cells_t + jnp.where(stencil[k] == row_ids, weight[k], 0.0)
+    natural = lax.broadcasted_iota(jnp.int32, (768, 768), 1)
+    place = lax.broadcasted_iota(jnp.int32, (768, 768), 0)
+    cell_of = jnp.where(
+        place < 512,
+        lax.shift_right_logical(place, 3) * 12 + (place & 7),
+        lax.shift_right_logical(place - 512, 2) * 12 + 8 + (place & 3),
+    )
+    order = jnp.where(natural == cell_of, 1.0, 0.0).astype(BF16)
+    high, rest = split(cells_t)
+    middle = (cells_t - high.astype(F32)) - rest.astype(F32)
+    cells_mat[...] = (
+        dot(order, high, NT) + dot(order, rest, NT) + dot(order, middle.astype(BF16), NT)
+    )
+
+    slots = lax.broadcasted_iota(jnp.int32, (16, 768), 0)
+    slots = jnp.where(slots < 12, slots, slots - 4)
+    chosen = jnp.where(
+        lax.broadcasted_iota(jnp.int32, (16, 768), 1) == slots + 12 * me, 1.0, 0.0
+    ).astype(F32)
+    target[...] = jnp.zeros((16, 128), F32)
+    for slot in range(16):
+        cell = slot if slot < 12 else slot - 4
+        target[slot : slot + 1, :VARS] = observed[cell] - output_bias[...]
+    target[:, :VARS] = target[:, :VARS] - dot(chosen, prev[...], NT, lax.Precision.HIGHEST)
+    lanes = lax.broadcasted_iota(jnp.int32, (16, 12), 1)
+    cell_ids = lax.broadcasted_iota(jnp.int32, (16, 12), 0)
+    cell_ids = jnp.where(cell_ids < 12, cell_ids, cell_ids - 4)
+    area_column = jnp.sum(
+        jnp.where(lanes == cell_ids, area[...], 0.0), axis=1, keepdims=True
+    )
+    coefficient[...] = jnp.zeros((16, 128), F32)
+    coefficient[:, :VARS] = area_column * var[...]
+
+    pl.semaphore_wait(known.at[0], 3)
+    for peer in lines[1]:
+        signal(known.at[1], "member", peer)
+    own[0].wait_recv()
+    relay_right = copy(4, gathered.at[2 * left], 2 * left, right)
+    relay_right.start()
+    own[1].wait_recv()
+    relay_left = copy(5, gathered.at[2 * right + 1], 2 * right + 1, left)
+    relay_left.start()
+    pl.semaphore_wait(known.at[1], 3)
+    for peer in lines[2]:
+        signal(known.at[2], "member", peer)
+    output[VARS:] = jnp.zeros((128 - VARS, 1024), BF16)
+    for load in loads[7:]:
+        load.wait()
+    for each in own[2:] + [relay_right, relay_left]:
+        each.wait_recv()
 
     rows_low = gathered[...].reshape(128, 1024)
     rows = rows_low.astype(F32)
@@ -230,7 +230,7 @@
     through = through_all[:128] - average * through_all[128:129]
     through_high, through_low = split(through)
     stack = jnp.concatenate([through_high, through_low, through_high], axis=0)
-    cells = cells_ref[...]
+    cells = cells_mat[...]
     variance = jnp.sum(
         cells * dot(cells, gram, NN, lax.Precision.HIGHEST), axis=1, keepdims=True
     )
@@ -266,7 +266,7 @@
         active = act * (0.5 * jnp.tanh(0.5 * act) + 0.5)
         return dot(active.astype(BF16), output[...], NT)
 
-    pl.semaphore_wait(barrier, members + 1)
+    pl.semaphore_wait(known.at[2], 1)
 
     @pl.loop(0, 4)
     def _(step):
@@ -474,8 +474,8 @@
     out_ref[:16] = result_ref[2 * spot] + part_in[4].astype(F32) + part_in[3].astype(F32)
     out_ref[16:] = result_ref[2 * spot + 1] + part_in[2].astype(F32) + part_in[5].astype(F32)
 
-    for hop in hops:
-        hop.wait_send()
+    for each in own + [relay_right, relay_left] + hops:
+        each.wait_send()
     settle(forecast_out_a, cast_send.at[0])
     settle(forecast_out_b, cast_send.at[1])
     settle(cot_out_a, back_send.at[0])
@@ -498,23 +498,18 @@
     members = lax.axis_size("member")
     vmem = pltpu.VMEM
     dma = pltpu.SemaphoreType.DMA
-    outside = pl.BlockSpec(memory_space=pltpu.MemorySpace.HBM)
-    inside = pl.BlockSpec(memory_space=pltpu.VMEM)
-    staged = pl.pallas_call(
-        gather_kernel,
-        name="gather_rows",
-        out_shape=(
-            jax.ShapeDtypeStruct((8, 16, 1024), BF16),
-            jax.ShapeDtypeStruct((768, 128), F32),
-            jax.ShapeDtypeStruct((16, 128), F32),
-            jax.ShapeDtypeStruct((16, 128), F32),
-            jax.ShapeDtypeStruct((1024, 1024), BF16),
-            jax.ShapeDtypeStruct((1, 1024), F32),
-            jax.ShapeDtypeStruct((128, 1024), BF16),
-        ),
-        in_specs=[outside] * 11,
-        out_specs=(inside,) * 7,
+
+    def body(*refs):
+        step_kernel(members, *refs)
+
+    out = pl.pallas_call(
+        body,
+        name="decoder_step",
+        out_shape=jax.ShapeDtypeStruct((32, 1024), F32),
+        in_specs=[pl.BlockSpec(memory_space=pl.ANY)] * 11,
+        out_specs=pl.BlockSpec(memory_space=pltpu.VMEM),
         scratch_shapes=[
+            vmem((8, 16, 1024), BF16),
             vmem((3, 1, 768), jnp.int32),
             vmem((3, 1, 768), F32),
             vmem((112, 768), F32),
@@ -522,42 +517,12 @@
             vmem((1, 12), F32),
             vmem((1, 112), F32),
             vmem((1, 112), F32),
-            dma((11,)),
-            dma((6,)),
-            dma((6,)),
-        ],
-        compiler_params=pltpu.CompilerParams(
-            collective_id=0, has_side_effects=True, vmem_limit_bytes=16 << 20
-        ),
-    )(
-        *(
-            pltpu.with_memory_space_constraint(each, pltpu.MemorySpace.HBM)
-            for each in (
-                processor_latent.reshape(2, 16, 1024),
-                jnp.transpose(stencil_index, (1, 0, 2)),
-                jnp.transpose(interp_weight, (1, 0, 2)),
-                prev_state[0],
-                jnp.transpose(observed, (2, 0, 1)),
-                cell_area,
-                var_weight.reshape(1, -1),
-                output_bias.reshape(1, -1),
-                hidden_weight,
-                hidden_bias.reshape(1, -1),
-                output_weight.T,
-            )
-        )
-    )
-
-    def body(*refs):
-        score_kernel(members, *refs)
-
-    out = pl.pallas_call(
-        body,
-        name="score_step",
-        out_shape=jax.ShapeDtypeStruct((32, 1024), F32),
-        in_specs=[inside] * 7,
-        out_specs=inside,
-        scratch_shapes=[
+            vmem((1024, 1024), BF16),
+            vmem((1, 1024), F32),
+            vmem((128, 1024), BF16),
+            vmem((768, 128), F32),
+            vmem((16, 128), F32),
+            vmem((16, 128), F32),
             vmem((768, 384), BF16),
             vmem((128, 768), BF16),
             vmem((768, 1024), F32),
@@ -579,6 +544,10 @@
             vmem((8, 16, 1024), BF16),
             vmem((2, 16, 1024), BF16),
             vmem((6, 16, 1024), BF16),
+            dma((11,)),
+            pltpu.SemaphoreType.REGULAR((3,)),
+            dma((6,)),
+            dma((6,)),
             dma((2,)),
             dma((2,)),
             dma((2,)),
@@ -586,10 +555,20 @@
             dma((6,)),
             dma((6,)),
         ],
-        compiler_params=pltpu.CompilerParams(
-            collective_id=1, has_side_effects=True, vmem_limit_bytes=28 << 20
-        ),
-    )(*staged)
+        compiler_params=pltpu.CompilerParams(collective_id=0, has_side_effects=True),
+    )(
+        processor_latent.reshape(2, 16, 1024),
+        jnp.transpose(stencil_index, (1, 0, 2)),
+        jnp.transpose(interp_weight, (1, 0, 2)),
+        prev_state[0],
+        jnp.transpose(observed, (2, 0, 1)),
+        cell_area,
+        var_weight.reshape(1, -1),
+        hidden_weight,
+        hidden_bias.reshape(1, -1),
+        output_weight.T,
+        output_bias.reshape(1, -1),
+    )
     return out[None]
 
 

time: 50.1 us -> 48.4 us (0.966)
  Pallas kernels: 48.8 us -> 46.7 us
  local copies, waits for them, and re-layouts: 0.66 us -> 1.57 us
    pallas_call x2 -> x1, Pallas kernels: 48.8 us -> 46.7 us  [local(): pl.pallas_call(body, name='decoder_step', out_shape=jax.ShapeDtypeStruct(...]
    unnamed x1, local copies, waits for them, and re-layouts: 0.66 us -> 1.57 us
where the time goes in v3:
time: 48.4 us; the launch traced here: 48.3 us
  Pallas kernels  46.7 us (96%)
  local copies, waits for them, and re-layouts  1.57 us (3%)
    pallas_call x1, Pallas kernels, local(): pl.pallas_call(body, name='decoder_step', out_shape=jax.ShapeDtypeStruct(...  46.7 us
    unnamed x1, local copies, waits for them, and re-layouts  1.57 us

profile of v3, /device:TPU:2, one launch (start us, length us, event | category | flops | bytes accessed | tf_op | source)
XLA Modules:
  0.0 48.3 jit_solution(11217037143046974076)
XLA Ops:
  0.0 46.7 %decoder_step.1 = f32[32,1024]{1,0:T(8,128)} custom-call(bf16[2,16,1024]{2,1,0:T(8,128)(2,1)} %bitcast.13, s32[3,1,768]{2,1,0:T(1,128)} %bitcast.14, f32[3,1,768]{2,1,0:T(1,128)} %bitcast.15, f32[112,768]{1,0:T(8,128)} %bitcast.11, f32[12,1,112]{2,1,0:T(1,128)} %bitcast.16, f32[1,12]{1,0:T(1,128)} %refs_5_.1, f32[1,112]{1,0:T(1,128)} %bitcast.18, ...), custom_call_target="tpu_custom_call" | custom-call | tf_op jit(solution)/shard_map/decoder_step/pallas_call | solution.py:505
  46.7 1.6 %copy.13 = f32[1,32,1024]{2,1,0:T(8,128)} copy(f32[1,32,1024]{2,1,0:T(8,128)} %bitcast.10) | data formatting | bytes 262144

commit v4 on v3

--- a/solution.py
+++ b/solution.py
@@ -74,7 +74,8 @@
     hidden,
     hidden_bias,
     output,
-    cells_mat,
+    inverse_ref,
+    stack,
     target,
     coefficient,
     blend,
@@ -175,11 +176,11 @@
         lax.shift_right_logical(place - 512, 2) * 12 + 8 + (place & 3),
     )
     order = jnp.where(natural == cell_of, 1.0, 0.0).astype(BF16)
-    high, rest = split(cells_t)
-    middle = (cells_t - high.astype(F32)) - rest.astype(F32)
-    cells_mat[...] = (
-        dot(order, high, NT) + dot(order, rest, NT) + dot(order, middle.astype(BF16), NT)
-    )
+    cells_high = cells_t.astype(BF16)
+    ordered = dot(order, cells_high, NT).astype(BF16)
+    blend[:, :128] = ordered
+    blend[:, 128:] = ordered
+    blend_t[...] = dot(cells_high, order, NT).astype(BF16)
 
     slots = lax.broadcasted_iota(jnp.int32, (16, 768), 0)
     slots = jnp.where(slots < 12, slots, slots - 4)
@@ -229,16 +230,11 @@
     )
     through = through_all[:128] - average * through_all[128:129]
     through_high, through_low = split(through)
-    stack = jnp.concatenate([through_high, through_low, through_high], axis=0)
-    cells = cells_mat[...]
-    variance = jnp.sum(
-        cells * dot(cells, gram, NN, lax.Precision.HIGHEST), axis=1, keepdims=True
-    )
-    scaled = cells * lax.rsqrt(variance + epsilon)
-    scaled_high, scaled_low = split(scaled)
-    blend[:, :128] = scaled_high
-    blend[:, 128:256] = scaled_high
-    blend[:, 256:] = scaled_low
+    stack[:128, :1024] = through_high
+    stack[128:, :1024] = through_low
+    gram_high, gram_low = split(gram)
+    stack[:128, 1024:] = gram_high
+    stack[128:, 1024:] = gram_low
 
     def exchange(source, place, to, send, recv):
         return pltpu.make_async_remote_copy(
@@ -250,19 +246,28 @@
             device_id_type=MESH_ID,
         )
 
-    def send_forecast(source, place, number, first, count):
-        @pl.loop(0, count)
-        def _(offset):
+    def send_forecast(source, place, number, first, count, apart):
+        def start(offset):
             to = first + lax.rem(me + 1 + offset, count)
-
-            @pl.when(to != me)
-            def _():
-                exchange(source, place, to, cast_send.at[number], cast_recv.at[number]).start()
+            exchange(source, place, to, cast_send.at[number], cast_recv.at[number]).start()
+
+        for offset in range(count - 1):
+            start(offset)
+
+        @pl.when(apart)
+        def _():
+            start(count - 1)
 
     def updates(span):
-        raw = dot(blend[span], stack, NN)
-        product[span] = raw
-        act = raw + hidden_bias[...]
+        raw = dot(blend[span], stack[...], NN)
+        variance = jnp.sum(
+            raw[:, 1024:] * blend[span, :128].astype(F32), axis=1, keepdims=True
+        )
+        inverse = lax.rsqrt(variance + epsilon)
+        inverse_ref[span] = jnp.broadcast_to(inverse, (128, 128))
+        value = raw[:, :1024] * inverse
+        product[span] = value
+        act = value + hidden_bias[...]
         active = act * (0.5 * jnp.tanh(0.5 * act) + 0.5)
         return dot(active.astype(BF16), output[...], NT)
 
@@ -273,7 +278,7 @@
         part = lax.rem(lax.div(me, 16) + 1 + step, 4)
         update = updates(pl.ds(pl.multiple_of(part * 128, 128), 128))
         forecast_out_a[pl.ds(part * 16, 16)] = update.reshape(16, 8, 128)
-        send_forecast(forecast_out_a, forecast_in_a, 0, part * 16, 16)
+        send_forecast(forecast_out_a, forecast_in_a, 0, part * 16, 16, step < 3)
 
     @pl.loop(0, 2)
     def _(step):
@@ -281,18 +286,17 @@
         update = updates(pl.ds(pl.multiple_of(512 + part * 128, 128), 128))
         for piece in range(32):
             forecast_out_b[part * 32 + piece] = update[piece * 4 : piece * 4 + 4]
-        send_forecast(forecast_out_b, forecast_in_b, 1, part * 32, 32)
+        send_forecast(forecast_out_b, forecast_in_b, 1, part * 32, 32, step < 1)
 
     forecast_in_a[me] = forecast_out_a[me]
     forecast_in_b[me] = forecast_out_b[me]
-    blend_t[...] = blend[:, :128].astype(F32).T.astype(BF16)
 
     @pl.loop(0, 6)
     def _(part):
         span = pl.ds(pl.multiple_of(part * 128, 128), 128)
         act = product[span] + hidden_bias[...]
         gate = 0.5 * jnp.tanh(0.5 * act) + 0.5
-        slope_act[span] = gate * (1.0 + act * (1.0 - gate))
+        slope_act[span] = gate * (1.0 + act * (1.0 - gate)) * inverse_ref[span][:, :1]
 
     others = pl.ds(0, members - 1)
 
@@ -342,10 +346,27 @@
                 * (slope(forecast_in_a[m] - target[:8]) - pair_factor * sums_a[m])
             ).astype(BF16)
 
+    core = lax.rem(me, 2)
+    row_y = lax.rem(lax.div(me, 2), 4)
+    row_x = lax.rem(lax.div(me, 8), 4)
+    row_z = lax.div(me, 32)
+    xs = [8 * lax.rem(row_x + step, 4) for step in range(4)]
+    ys = [2 * lax.rem(row_y + step, 4) for step in range(4)]
+    zs = [32 * row_z, 32 * (1 - row_z)]
+    cs = [core, 1 - core]
+    moves = [
+        (z + min(x, 4 - x) + min(y, 4 - y), z, x, y, c)
+        for z in range(2)
+        for x in range(4)
+        for y in range(4)
+        for c in range(2)
+        if z + x + y + c
+    ]
+    moves.sort(key=lambda move: -move[0])
+
     def send_back(source, place, number):
-        @pl.loop(1, members)
-        def _(offset):
-            to = lax.rem(me + offset, members)
+        for _, z, x, y, c in moves:
+            to = zs[z] + xs[x] + ys[y] + cs[c]
             exchange(source, place, to, back_send.at[number], back_recv.at[number]).start()
 
     send_back(cot_out_a, cot_in_a, 0)
@@ -415,7 +436,9 @@
         grad = dot(cot, output[...], NN) * slope_act[span]
         grad_side[span, :1024] = grad.astype(BF16)
         along = jnp.sum(grad * product[span], axis=1, keepdims=True) * (1.0 / 1024)
-        grad_side[span, 1024:] = (blend[span, :128].astype(F32) * along).astype(BF16)
+        grad_side[span, 1024:] = (
+            blend[span, :128].astype(F32) * (inverse_ref[span] * along)
+        ).astype(BF16)
 
     settle(cot_in_a, back_recv.at[0])
 
@@ -521,9 +544,10 @@
             vmem((1, 1024), F32),
             vmem((128, 1024), BF16),
             vmem((768, 128), F32),
+            vmem((256, 1152), BF16),
             vmem((16, 128), F32),
             vmem((16, 128), F32),
-            vmem((768, 384), BF16),
+            vmem((768, 256), BF16),
             vmem((128, 768), BF16),
             vmem((768, 1024), F32),
             vmem((768, 1024), F32),
@@ -555,19 +579,26 @@
             dma((6,)),
             dma((6,)),
         ],
-        compiler_params=pltpu.CompilerParams(collective_id=0, has_side_effects=True),
+        compiler_params=pltpu.CompilerParams(
+            collective_id=0, has_side_effects=True, vmem_limit_bytes=40 << 20
+        ),
     )(
-        processor_latent.reshape(2, 16, 1024),
-        jnp.transpose(stencil_index, (1, 0, 2)),
-        jnp.transpose(interp_weight, (1, 0, 2)),
-        prev_state[0],
-        jnp.transpose(observed, (2, 0, 1)),
-        cell_area,
-        var_weight.reshape(1, -1),
-        hidden_weight,
-        hidden_bias.reshape(1, -1),
-        output_weight.T,
-        output_bias.reshape(1, -1),
+        *(
+            pltpu.with_memory_space_constraint(each, pltpu.MemorySpace.HBM)
+            for each in (
+                processor_latent.reshape(2, 16, 1024),
+                jnp.transpose(stencil_index, (1, 0, 2)),
+                jnp.transpose(interp_weight, (1, 0, 2)),
+                prev_state[0],
+                jnp.transpose(observed, (2, 0, 1)),
+                cell_area,
+                var_weight.reshape(1, -1),
+                hidden_weight,
+                hidden_bias.reshape(1, -1),
+                output_weight.T,
+                output_bias.reshape(1, -1),
+            )
+        )
     )
     return out[None]
 

time: 48.4 us -> 45.4 us (0.938)
  Pallas kernels: 46.7 us -> 44.3 us
  local copies, waits for them, and re-layouts: 1.57 us -> 0.66 us
    pallas_call x1, Pallas kernels: 46.7 us -> 44.3 us  [local(): pl.pallas_call(body, name='decoder_step', out_shape=jax.ShapeDtypeStruct(...]
    unnamed x1, local copies, waits for them, and re-layouts: 1.57 us -> 0.66 us
where the time goes in v4:
time: 45.4 us; the launch traced here: 45 us
  Pallas kernels  44.3 us (98%)
  local copies, waits for them, and re-layouts  0.66 us (1%)
    pallas_call x1, Pallas kernels, local(): pl.pallas_call(body, name='decoder_step', out_shape=jax.ShapeDtypeStruct(...  44.3 us

profile of v4, /device:TPU:2, one launch (start us, length us, event | category | flops | bytes accessed | tf_op | source)
XLA Modules:
  0.0 45.0 jit_solution(5176810910191469281)
XLA Ops:
  0.0 44.3 %decoder_step.1 = f32[32,1024]{1,0:T(8,128)S(1)} custom-call(bf16[2,16,1024]{2,1,0:T(8,128)(2,1)} %bitcast.13, s32[3,1,768]{2,1,0:T(1,128)} %bitcast.14, f32[3,1,768]{2,1,0:T(1,128)} %bitcast.15, f32[112,768]{1,0:T(8,128)} %bitcast.11, f32[12,1,112]{2,1,0:T(1,128)} %bitcast.16, f32[1,12]{1,0:T(1,128)} %refs_5_.1, f32[1,112]{1,0:T(1,128)} %bitcast.18, ...), custom_call_target="tpu_custom_call" | custom-call | tf_op jit(solution)/shard_map/decoder_step/pallas_call | solution.py:528
  44.3 0.7 %copy.13 = f32[1,32,1024]{2,1,0:T(8,128)} copy(f32[1,32,1024]{2,1,0:T(8,128)S(1)} %bitcast.10) | data formatting | bytes 262144

commit v5 on v4

--- a/solution.py
+++ b/solution.py
@@ -137,8 +137,6 @@
             )
         )
     ]
-    for load in loads:
-        load.start()
     pl.semaphore_wait(barrier, 10)
     for peer in lines[0]:
         signal(known.at[0], "member", peer)
@@ -161,6 +159,8 @@
     ]
     for each in own:
         each.start()
+    for load in loads:
+        load.start()
     for load in loads[:7]:
         load.wait()
 
@@ -170,11 +170,13 @@
         cells_t = cells_t + jnp.where(stencil[k] == row_ids, weight[k], 0.0)
     natural = lax.broadcasted_iota(jnp.int32, (768, 768), 1)
     place = lax.broadcasted_iota(jnp.int32, (768, 768), 0)
-    cell_of = jnp.where(
+    slot = jnp.where(
         place < 512,
-        lax.shift_right_logical(place, 3) * 12 + (place & 7),
-        lax.shift_right_logical(place - 512, 2) * 12 + 8 + (place & 3),
+        lax.shift_right_logical(place, 3),
+        lax.shift_right_logical(place - 512, 2),
     )
+    scorer = 2 * (slot & 31) + lax.shift_right_logical(slot, 5)
+    cell_of = scorer * 12 + jnp.where(place < 512, place & 7, 8 + (place & 3))
     order = jnp.where(natural == cell_of, 1.0, 0.0).astype(BF16)
     cells_high = cells_t.astype(BF16)
     ordered = dot(order, cells_high, NT).astype(BF16)
@@ -236,27 +238,57 @@
     stack[:128, 1024:] = gram_high
     stack[128:, 1024:] = gram_low
 
-    def exchange(source, place, to, send, recv):
-        return pltpu.make_async_remote_copy(
-            src_ref=source.at[to],
-            dst_ref=place.at[me],
+    core = lax.rem(me, 2)
+    chip = lax.div(me, 2)
+    my_slot = core * 32 + chip
+    row_y = lax.rem(chip, 4)
+    row_x = lax.rem(lax.div(chip, 4), 4)
+    row_z = lax.div(chip, 16)
+    xs = [4 * lax.rem(row_x + step, 4) for step in range(4)]
+    ys = [lax.rem(row_y + step, 4) for step in range(4)]
+    zs = [16 * row_z, 16 * (1 - row_z)]
+    moves = [
+        (z + min(x, 4 - x) + min(y, 4 - y), z, x, y)
+        for z in range(2)
+        for x in range(4)
+        for y in range(4)
+        if z + x + y
+    ]
+    moves.sort(key=lambda move: -move[0])
+    chips = [zs[z] + xs[x] + ys[y] for _, z, x, y in moves]
+
+    def exchange(source, source_slot, place, place_slot, to, send, recv):
+        pltpu.make_async_remote_copy(
+            src_ref=source.at[source_slot],
+            dst_ref=place.at[place_slot],
             send_sem=send,
             recv_sem=recv,
             device_id={"member": to},
             device_id_type=MESH_ID,
-        )
-
-    def send_forecast(source, place, number, first, count, apart):
-        def start(offset):
-            to = first + lax.rem(me + 1 + offset, count)
-            exchange(source, place, to, cast_send.at[number], cast_recv.at[number]).start()
-
-        for offset in range(count - 1):
-            start(offset)
-
-        @pl.when(apart)
-        def _():
-            start(count - 1)
+        ).start()
+
+    def send_forecast(source, place, number, sides):
+        def start(other, side):
+            exchange(
+                source,
+                side * 32 + other,
+                place,
+                me,
+                2 * other + side,
+                cast_send.at[number],
+                cast_recv.at[number],
+            )
+
+        for other in chips:
+            for side in sides:
+                start(other, side)
+        if len(sides) == 2:
+            start(chip, 1 - core)
+        else:
+
+            @pl.when(core != sides[0])
+            def _():
+                start(chip, sides[0])
 
     def updates(span):
         raw = dot(blend[span], stack[...], NN)
@@ -264,7 +296,7 @@
             raw[:, 1024:] * blend[span, :128].astype(F32), axis=1, keepdims=True
         )
         inverse = lax.rsqrt(variance + epsilon)
-        inverse_ref[span] = jnp.broadcast_to(inverse, (128, 128))
+        inverse_ref[span] = jnp.broadcast_to(inverse, (256, 128))
         value = raw[:, :1024] * inverse
         product[span] = value
         act = value + hidden_bias[...]
@@ -273,23 +305,18 @@
 
     pl.semaphore_wait(known.at[2], 1)
 
-    @pl.loop(0, 4)
-    def _(step):
-        part = lax.rem(lax.div(me, 16) + 1 + step, 4)
-        update = updates(pl.ds(pl.multiple_of(part * 128, 128), 128))
-        forecast_out_a[pl.ds(part * 16, 16)] = update.reshape(16, 8, 128)
-        send_forecast(forecast_out_a, forecast_in_a, 0, part * 16, 16, step < 3)
-
-    @pl.loop(0, 2)
-    def _(step):
-        part = lax.rem(lax.div(me, 32) + 1 + step, 2)
-        update = updates(pl.ds(pl.multiple_of(512 + part * 128, 128), 128))
-        for piece in range(32):
-            forecast_out_b[part * 32 + piece] = update[piece * 4 : piece * 4 + 4]
-        send_forecast(forecast_out_b, forecast_in_b, 1, part * 32, 32, step < 1)
-
-    forecast_in_a[me] = forecast_out_a[me]
-    forecast_in_b[me] = forecast_out_b[me]
+    for side in range(2):
+        update = updates(pl.ds(side * 256, 256))
+        forecast_out_a[pl.ds(side * 32, 32)] = update.reshape(32, 8, 128)
+        send_forecast(forecast_out_a, forecast_in_a, 0, (side,))
+
+    update = updates(pl.ds(512, 256))
+    for piece in range(64):
+        forecast_out_b[piece] = update[piece * 4 : piece * 4 + 4]
+    send_forecast(forecast_out_b, forecast_in_b, 1, (0, 1))
+
+    forecast_in_a[me] = forecast_out_a[my_slot]
+    forecast_in_b[me] = forecast_out_b[my_slot]
 
     @pl.loop(0, 6)
     def _(part):
@@ -318,22 +345,30 @@
         for i in range(8):
             sums_a[base + i] = totals[i]
 
-    @pl.loop(0, 28)
-    def _(step):
-        first = lax.rem(step, 8) * 8
-        second = lax.rem(lax.rem(step, 8) + lax.div(step, 8) + 1, 8) * 8
+    def pair_blocks(first, seconds):
         values = [forecast_in_a[first + i] for i in range(8)]
         totals = [sums_a[first + i] for i in range(8)]
-        for j in range(8):
-            other = forecast_in_a[second + j]
-            total = sums_a[second + j]
-            for i in range(8):
-                push = slope(values[i] - other)
-                totals[i] = totals[i] + push
-                total = total - push
-            sums_a[second + j] = total
+        for second in seconds:
+            for j in range(8):
+                other = forecast_in_a[second + j]
+                total = sums_a[second + j]
+                for i in range(8):
+                    push = slope(values[i] - other)
+                    totals[i] = totals[i] + push
+                    total = total - push
+                sums_a[second + j] = total
         for i in range(8):
             sums_a[first + i] = totals[i]
+
+    @pl.loop(0, 12)
+    def _(step):
+        block = lax.rem(step, 8)
+        apart = block + 1 + 2 * lax.div(step, 8)
+        pair_blocks(block * 8, (lax.rem(apart, 8) * 8, lax.rem(apart + 1, 8) * 8))
+
+    @pl.loop(4, 8)
+    def _(block):
+        pair_blocks(block * 8, (lax.rem(block + 3, 8) * 8,))
 
     pair_factor = (1.0 - (1.0 - fairness) / members) / (members - 1)
 
@@ -346,31 +381,17 @@
                 * (slope(forecast_in_a[m] - target[:8]) - pair_factor * sums_a[m])
             ).astype(BF16)
 
-    core = lax.rem(me, 2)
-    row_y = lax.rem(lax.div(me, 2), 4)
-    row_x = lax.rem(lax.div(me, 8), 4)
-    row_z = lax.div(me, 32)
-    xs = [8 * lax.rem(row_x + step, 4) for step in range(4)]
-    ys = [2 * lax.rem(row_y + step, 4) for step in range(4)]
-    zs = [32 * row_z, 32 * (1 - row_z)]
-    cs = [core, 1 - core]
-    moves = [
-        (z + min(x, 4 - x) + min(y, 4 - y), z, x, y, c)
-        for z in range(2)
-        for x in range(4)
-        for y in range(4)
-        for c in range(2)
-        if z + x + y + c
-    ]
-    moves.sort(key=lambda move: -move[0])
-
     def send_back(source, place, number):
-        for _, z, x, y, c in moves:
-            to = zs[z] + xs[x] + ys[y] + cs[c]
-            exchange(source, place, to, back_send.at[number], back_recv.at[number]).start()
+        def start(to):
+            exchange(source, to, place, my_slot, to, back_send.at[number], back_recv.at[number])
+
+        for other in chips:
+            for side in range(2):
+                start(2 * other + side)
+        start(2 * chip + 1 - core)
 
     send_back(cot_out_a, cot_in_a, 0)
-    cot_in_a[me] = cot_out_a[me]
+    cot_in_a[my_slot] = cot_out_a[me]
 
     settle(forecast_in_b, cast_recv.at[1])
     for m in range(32):
@@ -430,7 +451,7 @@
             cot_out_b[m + 32] = cot[4:].astype(BF16)
 
     send_back(cot_out_b, cot_in_b, 1)
-    cot_in_b[me] = cot_out_b[me]
+    cot_in_b[my_slot] = cot_out_b[me]
 
     def backward(cot, span):
         grad = dot(cot, output[...], NN) * slope_act[span]

time: 45.4 us -> 44.6 us (0.982)
  Pallas kernels: 44.3 us -> 43.3 us
    pallas_call x1, Pallas kernels: 44.3 us -> 43.3 us  [local(): pl.pallas_call(body, name='decoder_step', out_shape=jax.ShapeDtypeStruct(...]
where the time goes in v5:
time: 44.6 us; the launch traced here: 43.9 us
  Pallas kernels  43.3 us (97%)
  local copies, waits for them, and re-layouts  0.66 us (1%)
    pallas_call x1, Pallas kernels, local(): pl.pallas_call(body, name='decoder_step', out_shape=jax.ShapeDtypeStruct(...  43.3 us

profile of v5, /device:TPU:2, one launch (start us, length us, event | category | flops | bytes accessed | tf_op | source)
XLA Modules:
  0.0 43.9 jit_solution(11280273096559787606)
XLA Ops:
  0.0 43.3 %decoder_step.1 = f32[32,1024]{1,0:T(8,128)S(1)} custom-call(bf16[2,16,1024]{2,1,0:T(8,128)(2,1)} %bitcast.13, s32[3,1,768]{2,1,0:T(1,128)} %bitcast.14, f32[3,1,768]{2,1,0:T(1,128)} %bitcast.15, f32[112,768]{1,0:T(8,128)} %bitcast.11, f32[12,1,112]{2,1,0:T(1,128)} %bitcast.16, f32[1,12]{1,0:T(1,128)} %refs_5_.1, f32[1,112]{1,0:T(1,128)} %bitcast.18, ...), custom_call_target="tpu_custom_call" | custom-call | tf_op jit(solution)/shard_map/decoder_step/pallas_call | solution.py:549
  43.3 0.7 %copy.13 = f32[1,32,1024]{2,1,0:T(8,128)} copy(f32[1,32,1024]{2,1,0:T(8,128)S(1)} %bitcast.10) | data formatting | bytes 262144

commit v6 on v5

--- a/solution.py
+++ b/solution.py
@@ -76,6 +76,8 @@
     output,
     inverse_ref,
     stack,
+    column_sums,
+    average_row,
     target,
     coefficient,
     blend,
@@ -230,6 +232,11 @@
     through_all = dot(
         jnp.concatenate([rows_low, jnp.ones((16, 1024), BF16)], axis=0), hidden[...], NN
     )
+    column_sums[...] = through_all[128:129]
+    diagonal = lax.broadcasted_iota(jnp.int32, (128, 128), 0) == lax.broadcasted_iota(
+        jnp.int32, (128, 128), 1
+    )
+    average_row[...] = jnp.sum(jnp.where(diagonal, average, 0.0), axis=0, keepdims=True)
     through = through_all[:128] - average * through_all[128:129]
     through_high, through_low = split(through)
     stack[:128, :1024] = through_high
@@ -481,44 +488,68 @@
     total = joined[...] + dot(blend_t[:, 512:], grad_side[512:], NN)
     outer = total[:, :1024].astype(BF16)
     inner = total[:, 1024:].astype(BF16)
-    result = dot(outer, hidden[...], NT)
-    result = result - dot(inner, gathered[...].reshape(128, 1024), NN)
-    result = result - jnp.mean(result, axis=1, keepdims=True)
-    result_ref[...] = result.reshape(8, 16, 1024)
-    part_out[...] = result.astype(BF16).reshape(8, 16, 1024)
-
-    def part_copy(number, source, to):
+    centre = jnp.sum(
+        outer.astype(F32) * column_sums[...], axis=1, keepdims=True
+    ) * (1.0 / 1024) - jnp.sum(inner.astype(F32) * average_row[...], axis=1, keepdims=True)
+
+    def part_copy(half, number, source, to):
         return pltpu.make_async_remote_copy(
             src_ref=source,
-            dst_ref=part_in.at[number],
-            send_sem=part_send.at[number],
-            recv_sem=part_recv.at[number],
+            dst_ref=part_in.at[half, number],
+            send_sem=part_send.at[half, number],
+            recv_sem=part_recv.at[half, number],
             device_id={"shard": to},
             device_id_type=MESH_ID,
         )
 
-    hops = [
-        part_copy(0, part_out.at[2 * across], right),
-        part_copy(1, part_out.at[2 * across + 1], left),
-        part_copy(2, part_out.at[2 * right + 1], right),
-        part_copy(3, part_out.at[2 * left], left),
-        part_copy(4, part_hop.at[0], right),
-        part_copy(5, part_hop.at[1], left),
-    ]
-    for hop in hops[:4]:
-        hop.start()
-    hops[0].wait_recv()
-    part_hop[0] = (part_in[0].astype(F32) + result_ref[2 * right]).astype(BF16)
-    hops[4].start()
-    hops[1].wait_recv()
-    part_hop[1] = (part_in[1].astype(F32) + result_ref[2 * left + 1]).astype(BF16)
-    hops[5].start()
-    for hop in hops[2:]:
-        hop.wait_recv()
-    out_ref[:16] = result_ref[2 * spot] + part_in[4].astype(F32) + part_in[3].astype(F32)
-    out_ref[16:] = result_ref[2 * spot + 1] + part_in[2].astype(F32) + part_in[5].astype(F32)
-
-    for each in own + [relay_right, relay_left] + hops:
+    halves = []
+    for half in range(2):
+        wide = slice(half * 512, half * 512 + 512)
+        result = dot(outer, hidden[wide], NT)
+        result = result - dot(inner, gathered[:, :, wide].reshape(128, 512), NN) - centre
+        result_ref[half] = result.reshape(8, 16, 512)
+        part_out[half] = result.astype(BF16).reshape(8, 16, 512)
+        hops = [
+            part_copy(half, 0, part_out.at[half, 2 * across], right),
+            part_copy(half, 1, part_out.at[half, 2 * across + 1], left),
+            part_copy(half, 2, part_out.at[half, 2 * right + 1], right),
+            part_copy(half, 3, part_out.at[half, 2 * left], left),
+            part_copy(half, 4, part_hop.at[half, 0], right),
+            part_copy(half, 5, part_hop.at[half, 1], left),
+        ]
+        for hop in hops[:2]:
+            hop.start()
+        halves.append(hops)
+    for hops in halves:
+        for hop in hops[2:4]:
+            hop.start()
+    for half, hops in enumerate(halves):
+        hops[0].wait_recv()
+        part_hop[half, 0] = (
+            part_in[half, 0].astype(F32) + result_ref[half, 2 * right]
+        ).astype(BF16)
+        hops[4].start()
+        hops[1].wait_recv()
+        part_hop[half, 1] = (
+            part_in[half, 1].astype(F32) + result_ref[half, 2 * left + 1]
+        ).astype(BF16)
+        hops[5].start()
+    for half, hops in enumerate(halves):
+        wide = slice(half * 512, half * 512 + 512)
+        for hop in hops[2:]:
+            hop.wait_recv()
+        out_ref[:16, wide] = (
+            result_ref[half, 2 * spot]
+            + part_in[half, 4].astype(F32)
+            + part_in[half, 3].astype(F32)
+        )
+        out_ref[16:, wide] = (
+            result_ref[half, 2 * spot + 1]
+            + part_in[half, 2].astype(F32)
+            + part_in[half, 5].astype(F32)
+        )
+
+    for each in own + [relay_right, relay_left] + halves[0] + halves[1]:
         each.wait_send()
     settle(forecast_out_a, cast_send.at[0])
     settle(forecast_out_b, cast_send.at[1])
@@ -566,6 +597,8 @@
             vmem((128, 1024), BF16),
             vmem((768, 128), F32),
             vmem((256, 1152), BF16),
+            vmem((1, 1024), F32),
+            vmem((1, 128), F32),
             vmem((16, 128), F32),
             vmem((16, 128), F32),
             vmem((768, 256), BF16),
@@ -585,10 +618,10 @@
             vmem((64, 4, 128), BF16),
             vmem((64, 8, 128), BF16),
             vmem((64, 4, 128), BF16),
-            vmem((8, 16, 1024), F32),
-            vmem((8, 16, 1024), BF16),
-            vmem((2, 16, 1024), BF16),
-            vmem((6, 16, 1024), BF16),
+            vmem((2, 8, 16, 512), F32),
+            vmem((2, 8, 16, 512), BF16),
+            vmem((2, 2, 16, 512), BF16),
+            vmem((2, 6, 16, 512), BF16),
             dma((11,)),
             pltpu.SemaphoreType.REGULAR((3,)),
             dma((6,)),
@@ -597,8 +630,8 @@
             dma((2,)),
             dma((2,)),
             dma((2,)),
-            dma((6,)),
-            dma((6,)),
+            dma((2, 6)),
+            dma((2, 6)),
         ],
         compiler_params=pltpu.CompilerParams(
             collective_id=0, has_side_effects=True, vmem_limit_bytes=40 << 20

time: 44.6 us -> 44 us (0.987)
  Pallas kernels: 43.3 us -> 42.6 us
    pallas_call x1, Pallas kernels: 43.3 us -> 42.6 us  [local(): pl.pallas_call(body, name='decoder_step', out_shape=jax.ShapeDtypeStruct(...]
where the time goes in v6:
time: 44 us; the launch traced here: 43.2 us
  Pallas kernels  42.6 us (97%)
  local copies, waits for them, and re-layouts  0.66 us (2%)
    pallas_call x1, Pallas kernels, local(): pl.pallas_call(body, name='decoder_step', out_shape=jax.ShapeDtypeStruct(...  42.6 us

profile of v6, /device:TPU:2, one launch (start us, length us, event | category | flops | bytes accessed | tf_op | source)
XLA Modules:
  0.0 43.2 jit_solution(2499182716946867478)
XLA Ops:
  0.0 42.6 %decoder_step.1 = f32[32,1024]{1,0:T(8,128)S(1)} custom-call(bf16[2,16,1024]{2,1,0:T(8,128)(2,1)} %bitcast.13, s32[3,1,768]{2,1,0:T(1,128)} %bitcast.14, f32[3,1,768]{2,1,0:T(1,128)} %bitcast.15, f32[112,768]{1,0:T(8,128)} %bitcast.11, f32[12,1,112]{2,1,0:T(1,128)} %bitcast.16, f32[1,12]{1,0:T(1,128)} %refs_5_.1, f32[1,112]{1,0:T(1,128)} %bitcast.18, ...), custom_call_target="tpu_custom_call" | custom-call | tf_op jit(solution)/shard_map/decoder_step/pallas_call | solution.py:580
  42.6 0.7 %copy.13 = f32[1,32,1024]{2,1,0:T(8,128)} copy(f32[1,32,1024]{2,1,0:T(8,128)S(1)} %bitcast.10) | data formatting | bytes 262144

commit v7 on v6

--- a/solution.py
+++ b/solution.py
@@ -132,7 +132,7 @@
                 (area_in, area),
                 (var_in, var),
                 (output_bias_in, output_bias),
-                (mesh_in, gathered.at[pl.ds(2 * spot, 2)]),
+                (mesh_in, gathered.at[pl.ds(4 * spot, 4)]),
                 (hidden_in, hidden),
                 (hidden_bias_in, hidden_bias),
                 (output_in, output.at[pl.ds(0, VARS)]),
@@ -153,14 +153,11 @@
             device_id_type=MESH_ID,
         )
 
-    own = [
-        copy(0, mesh_in.at[0], 2 * spot, right),
-        copy(1, mesh_in.at[1], 2 * spot + 1, left),
-        copy(2, mesh_in.at[1], 2 * spot + 1, right),
-        copy(3, mesh_in.at[0], 2 * spot, left),
-    ]
-    for each in own:
-        each.start()
+    to_right = [copy(i, mesh_in.at[i], 4 * spot + i, right) for i in range(4)]
+    to_left = [copy(7 - i, mesh_in.at[i], 4 * spot + i, left) for i in (3, 2, 1, 0)]
+    for pair in zip(to_right, to_left):
+        for each in pair:
+            each.start()
     for load in loads:
         load.start()
     for load in loads[:7]:
@@ -208,19 +205,21 @@
     pl.semaphore_wait(known.at[0], 3)
     for peer in lines[1]:
         signal(known.at[1], "member", peer)
-    own[0].wait_recv()
-    relay_right = copy(4, gathered.at[2 * left], 2 * left, right)
-    relay_right.start()
-    own[1].wait_recv()
-    relay_left = copy(5, gathered.at[2 * right + 1], 2 * right + 1, left)
-    relay_left.start()
+    relays = []
+    for i in range(2):
+        to_right[i].wait_recv()
+        relays.append(copy(8 + i, gathered.at[4 * left + i], 4 * left + i, right))
+        relays[-1].start()
+        to_left[i].wait_recv()
+        relays.append(copy(10 + i, gathered.at[4 * right + 3 - i], 4 * right + 3 - i, left))
+        relays[-1].start()
     pl.semaphore_wait(known.at[1], 3)
     for peer in lines[2]:
         signal(known.at[2], "member", peer)
     output[VARS:] = jnp.zeros((128 - VARS, 1024), BF16)
     for load in loads[7:]:
         load.wait()
-    for each in own[2:] + [relay_right, relay_left]:
+    for each in to_right[2:] + to_left[2:] + relays:
         each.wait_recv()
 
     rows_low = gathered[...].reshape(128, 1024)
@@ -549,7 +548,7 @@
             + part_in[half, 5].astype(F32)
         )
 
-    for each in own + [relay_right, relay_left] + halves[0] + halves[1]:
+    for each in to_right + to_left + relays + halves[0] + halves[1]:
         each.wait_send()
     settle(forecast_out_a, cast_send.at[0])
     settle(forecast_out_b, cast_send.at[1])
@@ -584,7 +583,7 @@
         in_specs=[pl.BlockSpec(memory_space=pl.ANY)] * 11,
         out_specs=pl.BlockSpec(memory_space=pltpu.VMEM),
         scratch_shapes=[
-            vmem((8, 16, 1024), BF16),
+            vmem((16, 8, 1024), BF16),
             vmem((3, 1, 768), jnp.int32),
             vmem((3, 1, 768), F32),
             vmem((112, 768), F32),
@@ -624,8 +623,8 @@
             vmem((2, 6, 16, 512), BF16),
             dma((11,)),
             pltpu.SemaphoreType.REGULAR((3,)),
-            dma((6,)),
-            dma((6,)),
+            dma((12,)),
+            dma((12,)),
             dma((2,)),
             dma((2,)),
             dma((2,)),
@@ -640,7 +639,7 @@
         *(
             pltpu.with_memory_space_constraint(each, pltpu.MemorySpace.HBM)
             for each in (
-                processor_latent.reshape(2, 16, 1024),
+                processor_latent.reshape(4, 8, 1024),
                 jnp.transpose(stencil_index, (1, 0, 2)),
                 jnp.transpose(interp_weight, (1, 0, 2)),
                 prev_state[0],

time: 44 us -> 43.7 us (level)
  no operation moved by 1% of the time
where the time goes in v7:
time: 43.7 us; the launch traced here: 43 us
  Pallas kernels  42.3 us (97%)
  local copies, waits for them, and re-layouts  0.66 us (2%)
    pallas_call x1, Pallas kernels, local(): pl.pallas_call(body, name='decoder_step', out_shape=jax.ShapeDtypeStruct(...  42.3 us

profile of v7, /device:TPU:2, one launch (start us, length us, event | category | flops | bytes accessed | tf_op | source)
XLA Modules:
  0.0 43.0 jit_solution(14369929609016126530)
XLA Ops:
  0.0 42.3 %decoder_step.1 = f32[32,1024]{1,0:T(8,128)S(1)} custom-call(bf16[4,8,1024]{2,1,0:T(8,128)(2,1)} %bitcast.13, s32[3,1,768]{2,1,0:T(1,128)} %bitcast.14, f32[3,1,768]{2,1,0:T(1,128)} %bitcast.15, f32[112,768]{1,0:T(8,128)} %bitcast.11, f32[12,1,112]{2,1,0:T(1,128)} %bitcast.16, f32[1,12]{1,0:T(1,128)} %refs_5_.1, f32[1,112]{1,0:T(1,128)} %bitcast.18, ...), custom_call_target="tpu_custom_call" | custom-call | tf_op jit(solution)/shard_map/decoder_step/pallas_call | solution.py:579
  42.3 0.7 %copy.13 = f32[1,32,1024]{2,1,0:T(8,128)} copy(f32[1,32,1024]{2,1,0:T(8,128)S(1)} %bitcast.10) | data formatting | bytes 262144
